TPU v7x, 512 devices: a whole 4x4x16 slice. The times are simulated.
512 devices in a mesh: chan: 128 (over x, z_lo, y), cross: 4 (over z_hi, core).
Axes of the slice: x: 4, y: 4, z: 16 (z_hi: 2, z_lo: 8; z = z_hi * 8 + z_lo), core: 2. Of those that a mesh axis runs over, the one named last changes fastest.
Arguments:
- positions: float32 [2, 512, 64, 128], P(None, 'chan', 'cross'), may hold values from 0 to 1
- velocity: float32 [2, 512, 64, 128], P(None, 'chan', 'cross'), may hold values from -4 to 4
- density: float32 [512, 64, 128], P('chan', 'cross'), may hold values from 0.8 to 1.2
- counts: int32 [512, 64], P('chan', 'cross'), may hold values from 0 to 128, as said below
Outputs:
- new_fields: float32 [5, 512, 64, 128], P(None, 'chan', 'cross')
- lowest_density: float32 [], replicated
Inputs may be any that keep to these rules, and one draw needn't show every extreme that they name: `counts`: in every channel column the bins from cross index 0 up to some height hold particles and those above are empty; the height is 56 or more; the bins at cross index 0 hold 128 particles.
All inputs are finite; a program needn't handle non-finite values.
Results may differ from a plain program's by a relative error of at most 0.0001.
Values sent between devices are 32-bit elements; how exact they have to be, the bound alone decides.
No kernel may reach another device: no remote copies, remote signals or barrier semaphores. Data moves between devices by JAX's collectives and lax.ppermute only.
A program may use at most 64 MiB of HBM per device.

v0:
```python
import math

import jax
import jax.numpy as jnp
from jax import lax
from jax.sharding import PartitionSpec as P

FAR_SHIFT = 8.0
SOUND_SQ = 100.0
KERNEL_GRAD = 140.0 / math.pi
PARTICLE_MASS = 1.0 / 128.0
GRAVITY = 1.0
TIME_STEP = 0.025


def padded_2(x, sides, width, wrap):
    for axis, dim in sides:
        size, length = (lax.axis_size(axis), x.shape[dim])
        up = [(i, (i + 1) % size) for i in range(size if wrap else size - 1)]
        down = [(j, i) for i, j in up]
        last = lax.slice_in_dim(x, length - width, length, axis=dim)
        leading = lax.slice_in_dim(x, 0, width, axis=dim)
        before = lax.ppermute(last, axis, up)
        after = lax.ppermute(leading, axis, down)
        x = jnp.concatenate([before, x, after], axis=dim)
    return x


def pack_fields(positions, velocity, density, occupied):
    return jnp.stack(
        [
            (positions[0] + FAR_SHIFT) * occupied,
            (positions[1] + FAR_SHIFT) * occupied,
            velocity[0] * occupied,
            velocity[1] * occupied,
            density * occupied,
        ]
    )


def column_rates(window):
    bin_rows = window.shape[2] - 2
    centre = window[:, 1, 1 : bin_rows + 1]
    centre_pressure = SOUND_SQ * (centre[4] - 1.0)
    force_x = jnp.zeros_like(centre[0])
    force_y = jnp.zeros_like(centre[0])
    compress = jnp.zeros_like(centre[0])
    for offset_col in (-1, 0, 1):
        for offset_row in (-1, 0, 1):
            neighbour = window[:, 1 + offset_col, 1 + offset_row : 1 + offset_row + bin_rows]
            delta_x = centre[0][:, :, None] - neighbour[0][:, None, :] - offset_col
            delta_y = centre[1][:, :, None] - neighbour[1][:, None, :] - offset_row
            radius = jnp.sqrt(delta_x * delta_x + delta_y * delta_y)
            weight = jnp.maximum(1.0 - radius, 0.0) ** 3
            pressure = (
                centre_pressure[:, :, None] + SOUND_SQ * (neighbour[4][:, None, :] - 1.0)
            ) * weight
            force_x = force_x + jnp.sum(pressure * delta_x, axis=2)
            force_y = force_y + jnp.sum(pressure * delta_y, axis=2)
            closing = (centre[2][:, :, None] - neighbour[2][:, None, :]) * delta_x + (
                centre[3][:, :, None] - neighbour[3][:, None, :]
            ) * delta_y
            compress = compress + jnp.sum(weight * closing, axis=2)
    force_scale = KERNEL_GRAD * PARTICLE_MASS
    return jnp.stack(
        [force_scale * force_x, force_scale * force_y - GRAVITY, -force_scale * compress]
    )


def extend_rims(fields):
    along_loop = padded_2(fields, (("chan", 1),), 1, True)
    extended = padded_2(along_loop, (("cross", 2),), 1, False)
    return extended


def local_rates(fields):
    padded = extend_rims(fields)
    columns = jnp.arange(fields.shape[1], dtype=jnp.int32)

    def one_column(column):
        return column_rates(lax.dynamic_slice_in_dim(padded, column, 3, 1))

    per_column = lax.map(one_column, columns)
    return jnp.transpose(per_column, (1, 0, 2, 3))


def body(positions, velocity, density, counts):
    slot_index = jnp.arange(positions.shape[-1], dtype=jnp.int32)
    occupied = (slot_index[None, None, :] < counts[:, :, None]).astype(jnp.float32)
    fields = pack_fields(positions, velocity, density, occupied)
    first_rates = local_rates(fields)
    half_step = 0.5 * TIME_STEP
    predicted = (
        jnp.stack(
            [
                fields[0] + half_step * fields[2],
                fields[1] + half_step * fields[3],
                fields[2] + half_step * first_rates[0],
                fields[3] + half_step * first_rates[1],
                fields[4] + half_step * first_rates[2],
            ]
        )
        * occupied
    )
    second_rates = local_rates(predicted)
    final_ux = fields[2] + TIME_STEP * second_rates[0]
    final_uy = fields[3] + TIME_STEP * second_rates[1]
    final_x = fields[0] + half_step * (fields[2] + final_ux) - FAR_SHIFT
    final_y = fields[1] + half_step * (fields[3] + final_uy) - FAR_SHIFT
    final_density = fields[4] + TIME_STEP * second_rates[2]
    new_fields = jnp.stack([final_x, final_y, final_ux, final_uy, final_density]) * occupied
    own_lowest = jnp.min(jnp.where(occupied > 0.0, final_density, 1000000000.0))
    lowest = lax.pmin(own_lowest, ("chan", "cross"))
    return (new_fields, lowest)


def solution(mesh):
    return jax.shard_map(
        body,
        mesh=mesh,
        in_specs=(
            P(None, "chan", "cross", None),
            P(None, "chan", "cross", None),
            P("chan", "cross", None),
            P("chan", "cross"),
        ),
        out_specs=(P(None, "chan", "cross", None), P()),
        check_vma=False,
    )
```

profile of v0, /device:TPU:1, one launch (start us, length us, event | category | flops | bytes accessed | tf_op | source)
XLA Modules:
  0.0 367.3 jit_solution(17792203976654721422)
XLA Ops:
  0.7 0.9 constant_dynamic-update-slice_fusion.4
  1.8 0.7 copy-done.2
  2.6 4.0 %collective-permute-start = (f32[5,1,16,128]{3,2,1,0:T(8,128)S(1)}, f32[5,1,16,128]{3,2,1,0:T(8,128)S(1)}, u32[]{:S(2)}, u32[]{:S(2)}) collective-permute-start(f32[5,1,16,128]{3,2,1,0:T(8,128)S(1)} %get-tuple-element.374), channel_id=1, source_target_pairs={{0,4},{4,8},{8,12},{12,16},{16,20},{20,24},{24,28},{28,32},{32,36}... | collective-permute-start | bytes 122888 | tf_op jit(solution)/shard_map/ppermute | solution.py:23
  6.6 16.2 %collective-permute-start.1 = (f32[5,1,16,128]{3,2,1,0:T(8,128)S(1)}, f32[5,1,16,128]{3,2,1,0:T(8,128)S(1)}, u32[]{:S(2)}, u32[]{:S(2)}) collective-permute-start(f32[5,1,16,128]{3,2,1,0:T(8,128)S(1)} %get-tuple-element.375), channel_id=1, source_target_pairs={{4,0},{8,4},{12,8},{16,12},{20,16},{24,20},{28,24},{32,28},{36,32}... | collective-permute-start | bytes 122888 | tf_op jit(solution)/shard_map/ppermute | solution.py:24
  22.9 1.1 collective-permute-done.1
  24.0 13.8 %collective-permute-start.2 = (f32[5,6,1,128]{3,2,1,0:T(1,128)S(1)}, f32[5,6,1,128]{3,2,1,0:T(1,128)S(1)}, u32[]{:S(2)}, u32[]{:S(2)}) collective-permute-start(f32[5,6,1,128]{3,2,1,0:T(1,128)S(1)} %get-tuple-element.370), channel_id=1, source_target_pairs={{0,1},{1,2},{2,3},{4,5},{5,6},{6,7},{8,9},{9,10},{10,11},{12,13},{... | collective-permute-start | bytes 46088 | tf_op jit(solution)/shard_map/ppermute | solution.py:23
  37.8 1.9 collective-permute-start.3
  39.8 11.7 %collective-permute-done.3 = f32[5,6,1,128]{3,2,1,0:T(1,128)S(1)} collective-permute-done((f32[5,6,1,128]{3,2,1,0:T(1,128)S(1)}, f32[5,6,1,128]{3,2,1,0:T(1,128)S(1)}, u32[]{:S(2)}, u32[]{:S(2)}) %collective-permute-start.3) | collective-permute-done | bytes 15392 | tf_op jit(solution)/shard_map/ppermute | solution.py:24
  51.6 87.6 %while.26 = (s32[]{:T(128)}, f32[4,3,16,128]{3,2,0,1:T(8,128)S(1)}, s32[4]{0:T(128)S(1)}, f32[5,6,18,128]{3,2,1,0:T(8,128)S(1)}, s32[]{:T(128)}, /*index=5*/s32[...) while((s32[]{:T(128)}, f32[4,3,16,128]{3,2,0,1:T(8,128)S(1)}, s32[4]{0:T(128)S(1)}, ...), condition=%wide.region_28.29_spmd, body=%wide.region_0.28_spmd.sunk | while | flops 60606472 | bytes 1761539 | solution.py:83
  51.6 0.6 dynamic_slice.31
  54.4 5.4 %multiply_reduce_fusion.43 = (f32[16,128]{1,0:T(8,128)S(1)}, f32[16,128]{1,0:T(8,128)S(1)}, f32[16,128]{1,0:T(8,128)S(1)}, f32[16,128]{1,0:T(8,128)S(1)}, f32[16...) fusion(f32[16,128]{1,0:T(8,128)S(1)} %get-tuple-element.611, ...), kind=kLoop, calls=%fused_computation.94.clone.1 | loop fusion | flops 16498688 | bytes 212992 | tf_op jit(solution)/shard_map/while/body/eval_jaxpr/reduce_sum | solution.py:58
  59.8 5.3 %multiply_reduce_fusion.42 = (f32[16,128]{1,0:T(8,128)S(1)}, f32[16,128]{1,0:T(8,128)S(1)}, f32[16,128]{1,0:T(8,128)S(1)}, f32[16,128]{1,0:T(8,128)S(1)}, f32[16...) fusion(f32[16,128]{1,0:T(8,128)S(1)} %get-tuple-element.596, ...), kind=kLoop, calls=%fused_computation.101.clone.1 | loop fusion | flops 17025024 | bytes 212992 | tf_op jit(solution)/shard_map/while/body/eval_jaxpr/reduce_sum | solution.py:58
  65.1 6.7 %multiply_reduce_fusion.41 = (f32[16,128]{1,0:T(8,128)S(1)}, f32[16,128]{1,0:T(8,128)S(1)}, f32[16,128]{1,0:T(8,128)S(1)}, f32[16,128]{1,0:T(8,128)S(1)}, f32[16...) fusion(f32[16,128]{1,0:T(8,128)S(1)} %get-tuple-element.581, ...), kind=kLoop, calls=%fused_computation.98.clone.1 | loop fusion | flops 22523904 | bytes 237568 | tf_op jit(solution)/shard_map/while/body/eval_jaxpr/reduce_sum | solution.py:58
  71.8 1.6 multiply_reduce_fusion.40
  73.5 0.6 dynamic_slice.31
  76.3 5.4 %multiply_reduce_fusion.43 = (f32[16,128]{1,0:T(8,128)S(1)}, f32[16,128]{1,0:T(8,128)S(1)}, f32[16,128]{1,0:T(8,128)S(1)}, f32[16,128]{1,0:T(8,128)S(1)}, f32[16...) fusion(f32[16,128]{1,0:T(8,128)S(1)} %get-tuple-element.611, ...), kind=kLoop, calls=%fused_computation.94.clone.1 | loop fusion | flops 16498688 | bytes 212992 | tf_op jit(solution)/shard_map/while/body/eval_jaxpr/reduce_sum | solution.py:58
  81.7 5.3 %multiply_reduce_fusion.42 = (f32[16,128]{1,0:T(8,128)S(1)}, f32[16,128]{1,0:T(8,128)S(1)}, f32[16,128]{1,0:T(8,128)S(1)}, f32[16,128]{1,0:T(8,128)S(1)}, f32[16...) fusion(f32[16,128]{1,0:T(8,128)S(1)} %get-tuple-element.596, ...), kind=kLoop, calls=%fused_computation.101.clone.1 | loop fusion | flops 17025024 | bytes 212992 | tf_op jit(solution)/shard_map/while/body/eval_jaxpr/reduce_sum | solution.py:58
  87.0 6.7 %multiply_reduce_fusion.41 = (f32[16,128]{1,0:T(8,128)S(1)}, f32[16,128]{1,0:T(8,128)S(1)}, f32[16,128]{1,0:T(8,128)S(1)}, f32[16,128]{1,0:T(8,128)S(1)}, f32[16...) fusion(f32[16,128]{1,0:T(8,128)S(1)} %get-tuple-element.581, ...), kind=kLoop, calls=%fused_computation.98.clone.1 | loop fusion | flops 22523904 | bytes 237568 | tf_op jit(solution)/shard_map/while/body/eval_jaxpr/reduce_sum | solution.py:58
  93.7 1.6 multiply_reduce_fusion.40
  95.4 0.6 dynamic_slice.31
  97.9 0.2 fusion.230
  98.2 5.4 %multiply_reduce_fusion.43 = (f32[16,128]{1,0:T(8,128)S(1)}, f32[16,128]{1,0:T(8,128)S(1)}, f32[16,128]{1,0:T(8,128)S(1)}, f32[16,128]{1,0:T(8,128)S(1)}, f32[16...) fusion(f32[16,128]{1,0:T(8,128)S(1)} %get-tuple-element.611, ...), kind=kLoop, calls=%fused_computation.94.clone.1 | loop fusion | flops 16498688 | bytes 212992 | tf_op jit(solution)/shard_map/while/body/eval_jaxpr/reduce_sum | solution.py:58
  103.6 5.3 %multiply_reduce_fusion.42 = (f32[16,128]{1,0:T(8,128)S(1)}, f32[16,128]{1,0:T(8,128)S(1)}, f32[16,128]{1,0:T(8,128)S(1)}, f32[16,128]{1,0:T(8,128)S(1)}, f32[16...) fusion(f32[16,128]{1,0:T(8,128)S(1)} %get-tuple-element.596, ...), kind=kLoop, calls=%fused_computation.101.clone.1 | loop fusion | flops 17025024 | bytes 212992 | tf_op jit(solution)/shard_map/while/body/eval_jaxpr/reduce_sum | solution.py:58
  108.9 6.7 %multiply_reduce_fusion.41 = (f32[16,128]{1,0:T(8,128)S(1)}, f32[16,128]{1,0:T(8,128)S(1)}, f32[16,128]{1,0:T(8,128)S(1)}, f32[16,128]{1,0:T(8,128)S(1)}, f32[16...) fusion(f32[16,128]{1,0:T(8,128)S(1)} %get-tuple-element.581, ...), kind=kLoop, calls=%fused_computation.98.clone.1 | loop fusion | flops 22523904 | bytes 237568 | tf_op jit(solution)/shard_map/while/body/eval_jaxpr/reduce_sum | solution.py:58
  115.6 1.6 multiply_reduce_fusion.40
  117.3 0.6 dynamic_slice.31
  120.1 5.4 %multiply_reduce_fusion.43 = (f32[16,128]{1,0:T(8,128)S(1)}, f32[16,128]{1,0:T(8,128)S(1)}, f32[16,128]{1,0:T(8,128)S(1)}, f32[16,128]{1,0:T(8,128)S(1)}, f32[16...) fusion(f32[16,128]{1,0:T(8,128)S(1)} %get-tuple-element.611, ...), kind=kLoop, calls=%fused_computation.94.clone.1 | loop fusion | flops 16498688 | bytes 212992 | tf_op jit(solution)/shard_map/while/body/eval_jaxpr/reduce_sum | solution.py:58
  125.5 5.3 %multiply_reduce_fusion.42 = (f32[16,128]{1,0:T(8,128)S(1)}, f32[16,128]{1,0:T(8,128)S(1)}, f32[16,128]{1,0:T(8,128)S(1)}, f32[16,128]{1,0:T(8,128)S(1)}, f32[16...) fusion(f32[16,128]{1,0:T(8,128)S(1)} %get-tuple-element.596, ...), kind=kLoop, calls=%fused_computation.101.clone.1 | loop fusion | flops 17025024 | bytes 212992 | tf_op jit(solution)/shard_map/while/body/eval_jaxpr/reduce_sum | solution.py:58
  130.8 6.7 %multiply_reduce_fusion.41 = (f32[16,128]{1,0:T(8,128)S(1)}, f32[16,128]{1,0:T(8,128)S(1)}, f32[16,128]{1,0:T(8,128)S(1)}, f32[16,128]{1,0:T(8,128)S(1)}, f32[16...) fusion(f32[16,128]{1,0:T(8,128)S(1)} %get-tuple-element.581, ...), kind=kLoop, calls=%fused_computation.98.clone.1 | loop fusion | flops 22523904 | bytes 237568 | tf_op jit(solution)/shard_map/while/body/eval_jaxpr/reduce_sum | solution.py:58
  137.5 1.6 multiply_reduce_fusion.40
  139.5 1.9 collective-permute-start.4
  141.4 14.8 %collective-permute-start.5 = (f32[5,1,16,128]{3,2,1,0:T(8,128)S(1)}, f32[5,1,16,128]{3,2,1,0:T(8,128)S(1)}, u32[]{:S(2)}, u32[]{:S(2)}) collective-permute-start(f32[5,1,16,128]{3,2,1,0:T(8,128)S(1)} %get-tuple-element.373), channel_id=1, source_target_pairs={{4,0},{8,4},{12,8},{16,12},{20,16},{24,20},{28,24},{32,28},{36,32}... | collective-permute-start | bytes 122888 | tf_op jit(solution)/shard_map/ppermute | solution.py:24
  156.2 1.1 collective-permute-done.5
  157.3 2.8 collective-permute-start.6
  160.1 2.1 collective-permute-start.7
  162.2 11.6 %collective-permute-done.7 = f32[5,6,1,128]{3,2,1,0:T(1,128)S(1)} collective-permute-done((f32[5,6,1,128]{3,2,1,0:T(1,128)S(1)}, f32[5,6,1,128]{3,2,1,0:T(1,128)S(1)}, u32[]{:S(2)}, u32[]{:S(2)}) %collective-permute-start.7) | collective-permute-done | bytes 15392 | tf_op jit(solution)/shard_map/ppermute | solution.py:24
  173.9 87.6 %while.27 = (s32[]{:T(128)}, f32[4,3,16,128]{3,2,0,1:T(8,128)S(1)}, s32[4]{0:T(128)S(1)}, f32[5,6,18,128]{3,2,1,0:T(8,128)S(1)}, s32[]{:T(128)}, /*index=5*/s32[...) while((s32[]{:T(128)}, f32[4,3,16,128]{3,2,0,1:T(8,128)S(1)}, s32[4]{0:T(128)S(1)}, ...), condition=%wide.region_57.58_spmd, body=%wide.region_29.57_spmd.sunk | while | flops 60606472 | bytes 1761539 | solution.py:83
  173.9 0.6 dynamic_slice.32
  176.5 0.2 fusion.232
  176.7 5.4 %multiply_reduce_fusion.47 = (f32[16,128]{1,0:T(8,128)S(1)}, f32[16,128]{1,0:T(8,128)S(1)}, f32[16,128]{1,0:T(8,128)S(1)}, f32[16,128]{1,0:T(8,128)S(1)}, f32[16...) fusion(f32[16,128]{1,0:T(8,128)S(1)} %get-tuple-element.689, ...), kind=kLoop, calls=%fused_computation.312.clone.1 | loop fusion | flops 16498688 | bytes 212992 | tf_op jit(solution)/shard_map/while/body/eval_jaxpr/reduce_sum | solution.py:58
  182.1 5.3 %multiply_reduce_fusion.46 = (f32[16,128]{1,0:T(8,128)S(1)}, f32[16,128]{1,0:T(8,128)S(1)}, f32[16,128]{1,0:T(8,128)S(1)}, f32[16,128]{1,0:T(8,128)S(1)}, f32[16...) fusion(f32[16,128]{1,0:T(8,128)S(1)} %get-tuple-element.674, ...), kind=kLoop, calls=%fused_computation.319.clone.1 | loop fusion | flops 17025024 | bytes 212992 | tf_op jit(solution)/shard_map/while/body/eval_jaxpr/reduce_sum | solution.py:58
  187.4 6.7 %multiply_reduce_fusion.45 = (f32[16,128]{1,0:T(8,128)S(1)}, f32[16,128]{1,0:T(8,128)S(1)}, f32[16,128]{1,0:T(8,128)S(1)}, f32[16,128]{1,0:T(8,128)S(1)}, f32[16...) fusion(f32[16,128]{1,0:T(8,128)S(1)} %get-tuple-element.659, ...), kind=kLoop, calls=%fused_computation.316.clone.1 | loop fusion | flops 22523904 | bytes 237568 | tf_op jit(solution)/shard_map/while/body/eval_jaxpr/reduce_sum | solution.py:58
  194.1 1.6 multiply_reduce_fusion.44
  195.8 0.6 dynamic_slice.32
  198.4 0.2 fusion.232
  198.6 5.4 %multiply_reduce_fusion.47 = (f32[16,128]{1,0:T(8,128)S(1)}, f32[16,128]{1,0:T(8,128)S(1)}, f32[16,128]{1,0:T(8,128)S(1)}, f32[16,128]{1,0:T(8,128)S(1)}, f32[16...) fusion(f32[16,128]{1,0:T(8,128)S(1)} %get-tuple-element.689, ...), kind=kLoop, calls=%fused_computation.312.clone.1 | loop fusion | flops 16498688 | bytes 212992 | tf_op jit(solution)/shard_map/while/body/eval_jaxpr/reduce_sum | solution.py:58
  204.0 5.3 %multiply_reduce_fusion.46 = (f32[16,128]{1,0:T(8,128)S(1)}, f32[16,128]{1,0:T(8,128)S(1)}, f32[16,128]{1,0:T(8,128)S(1)}, f32[16,128]{1,0:T(8,128)S(1)}, f32[16...) fusion(f32[16,128]{1,0:T(8,128)S(1)} %get-tuple-element.674, ...), kind=kLoop, calls=%fused_computation.319.clone.1 | loop fusion | flops 17025024 | bytes 212992 | tf_op jit(solution)/shard_map/while/body/eval_jaxpr/reduce_sum | solution.py:58
  209.3 6.7 %multiply_reduce_fusion.45 = (f32[16,128]{1,0:T(8,128)S(1)}, f32[16,128]{1,0:T(8,128)S(1)}, f32[16,128]{1,0:T(8,128)S(1)}, f32[16,128]{1,0:T(8,128)S(1)}, f32[16...) fusion(f32[16,128]{1,0:T(8,128)S(1)} %get-tuple-element.659, ...), kind=kLoop, calls=%fused_computation.316.clone.1 | loop fusion | flops 22523904 | bytes 237568 | tf_op jit(solution)/shard_map/while/body/eval_jaxpr/reduce_sum | solution.py:58
  216.0 1.6 multiply_reduce_fusion.44
  217.7 0.6 dynamic_slice.32
  220.3 0.2 fusion.232
  220.5 5.4 %multiply_reduce_fusion.47 = (f32[16,128]{1,0:T(8,128)S(1)}, f32[16,128]{1,0:T(8,128)S(1)}, f32[16,128]{1,0:T(8,128)S(1)}, f32[16,128]{1,0:T(8,128)S(1)}, f32[16...) fusion(f32[16,128]{1,0:T(8,128)S(1)} %get-tuple-element.689, ...), kind=kLoop, calls=%fused_computation.312.clone.1 | loop fusion | flops 16498688 | bytes 212992 | tf_op jit(solution)/shard_map/while/body/eval_jaxpr/reduce_sum | solution.py:58
  225.9 5.3 %multiply_reduce_fusion.46 = (f32[16,128]{1,0:T(8,128)S(1)}, f32[16,128]{1,0:T(8,128)S(1)}, f32[16,128]{1,0:T(8,128)S(1)}, f32[16,128]{1,0:T(8,128)S(1)}, f32[16...) fusion(f32[16,128]{1,0:T(8,128)S(1)} %get-tuple-element.674, ...), kind=kLoop, calls=%fused_computation.319.clone.1 | loop fusion | flops 17025024 | bytes 212992 | tf_op jit(solution)/shard_map/while/body/eval_jaxpr/reduce_sum | solution.py:58
  231.2 6.7 %multiply_reduce_fusion.45 = (f32[16,128]{1,0:T(8,128)S(1)}, f32[16,128]{1,0:T(8,128)S(1)}, f32[16,128]{1,0:T(8,128)S(1)}, f32[16,128]{1,0:T(8,128)S(1)}, f32[16...) fusion(f32[16,128]{1,0:T(8,128)S(1)} %get-tuple-element.659, ...), kind=kLoop, calls=%fused_computation.316.clone.1 | loop fusion | flops 22523904 | bytes 237568 | tf_op jit(solution)/shard_map/while/body/eval_jaxpr/reduce_sum | solution.py:58
  237.9 1.6 multiply_reduce_fusion.44
  239.6 0.6 dynamic_slice.32
  242.2 0.2 fusion.232
  242.4 5.4 %multiply_reduce_fusion.47 = (f32[16,128]{1,0:T(8,128)S(1)}, f32[16,128]{1,0:T(8,128)S(1)}, f32[16,128]{1,0:T(8,128)S(1)}, f32[16,128]{1,0:T(8,128)S(1)}, f32[16...) fusion(f32[16,128]{1,0:T(8,128)S(1)} %get-tuple-element.689, ...), kind=kLoop, calls=%fused_computation.312.clone.1 | loop fusion | flops 16498688 | bytes 212992 | tf_op jit(solution)/shard_map/while/body/eval_jaxpr/reduce_sum | solution.py:58
  247.8 5.3 %multiply_reduce_fusion.46 = (f32[16,128]{1,0:T(8,128)S(1)}, f32[16,128]{1,0:T(8,128)S(1)}, f32[16,128]{1,0:T(8,128)S(1)}, f32[16,128]{1,0:T(8,128)S(1)}, f32[16...) fusion(f32[16,128]{1,0:T(8,128)S(1)} %get-tuple-element.674, ...), kind=kLoop, calls=%fused_computation.319.clone.1 | loop fusion | flops 17025024 | bytes 212992 | tf_op jit(solution)/shard_map/while/body/eval_jaxpr/reduce_sum | solution.py:58
  253.1 6.7 %multiply_reduce_fusion.45 = (f32[16,128]{1,0:T(8,128)S(1)}, f32[16,128]{1,0:T(8,128)S(1)}, f32[16,128]{1,0:T(8,128)S(1)}, f32[16,128]{1,0:T(8,128)S(1)}, f32[16...) fusion(f32[16,128]{1,0:T(8,128)S(1)} %get-tuple-element.659, ...), kind=kLoop, calls=%fused_computation.316.clone.1 | loop fusion | flops 22523904 | bytes 237568 | tf_op jit(solution)/shard_map/while/body/eval_jaxpr/reduce_sum | solution.py:58
  259.8 1.6 multiply_reduce_fusion.44
  261.6 0.7 select_reduce_fusion
  262.6 0.7 broadcast_multiply_fusion
  263.3 104.0 %pmin.7 = f32[]{:T(128)} all-reduce(f32[]{:T(128)} %select_reduce_fusion), channel_id=1, replica_groups=mesh['chan'=128,'cross'=4] {'chan','cross'}, use_global_device_ids=true, to_apply=%region_59.60 | all-reduce | flops 1 | bytes 8 | tf_op jit(solution)/shard_map/pmin | solution.py:113
  (62 shorter events, 2.3 us)
Async XLA Ops:
  0.6 0.9 copy-start.3
  0.6 0.9 copy-start.1
  0.6 1.0 copy-start
  1.7 0.8 copy-start.2
  2.6 20.3 %collective-permute-start = (f32[5,1,16,128]{3,2,1,0:T(8,128)S(1)}, f32[5,1,16,128]{3,2,1,0:T(8,128)S(1)}, u32[]{:S(2)}, u32[]{:S(2)}) collective-permute-start(f32[5,1,16,128]{3,2,1,0:T(8,128)S(1)} %get-tuple-element.374), channel_id=1, source_target_pairs={{0,4},{4,8},{8,12},{12,16},{16,20},{20,24},{24,28},{28,32},{32,36}... | collective-permute-start | bytes 122888 | tf_op jit(solution)/shard_map/ppermute | solution.py:23
  6.6 17.3 %collective-permute-start.1 = (f32[5,1,16,128]{3,2,1,0:T(8,128)S(1)}, f32[5,1,16,128]{3,2,1,0:T(8,128)S(1)}, u32[]{:S(2)}, u32[]{:S(2)}) collective-permute-start(f32[5,1,16,128]{3,2,1,0:T(8,128)S(1)} %get-tuple-element.375), channel_id=1, source_target_pairs={{4,0},{8,4},{12,8},{16,12},{20,16},{24,20},{28,24},{32,28},{36,32}... | collective-permute-start | bytes 122888 | tf_op jit(solution)/shard_map/ppermute | solution.py:24
  24.0 15.8 %collective-permute-start.2 = (f32[5,6,1,128]{3,2,1,0:T(1,128)S(1)}, f32[5,6,1,128]{3,2,1,0:T(1,128)S(1)}, u32[]{:S(2)}, u32[]{:S(2)}) collective-permute-start(f32[5,6,1,128]{3,2,1,0:T(1,128)S(1)} %get-tuple-element.370), channel_id=1, source_target_pairs={{0,1},{1,2},{2,3},{4,5},{5,6},{6,7},{8,9},{9,10},{10,11},{12,13},{... | collective-permute-start | bytes 46088 | tf_op jit(solution)/shard_map/ppermute | solution.py:23
  37.8 13.8 %collective-permute-start.3 = (f32[5,6,1,128]{3,2,1,0:T(1,128)S(1)}, f32[5,6,1,128]{3,2,1,0:T(1,128)S(1)}, u32[]{:S(2)}, u32[]{:S(2)}) collective-permute-start(f32[5,6,1,128]{3,2,1,0:T(1,128)S(1)} %get-tuple-element.371), channel_id=1, source_target_pairs={{1,0},{2,1},{3,2},{5,4},{6,5},{7,6},{9,8},{10,9},{11,10},{13,12},{... | collective-permute-start | bytes 46088 | tf_op jit(solution)/shard_map/ppermute | solution.py:24
  139.5 16.7 %collective-permute-start.4 = (f32[5,1,16,128]{3,2,1,0:T(8,128)S(1)}, f32[5,1,16,128]{3,2,1,0:T(8,128)S(1)}, u32[]{:S(2)}, u32[]{:S(2)}) collective-permute-start(f32[5,1,16,128]{3,2,1,0:T(8,128)S(1)} %get-tuple-element.372), channel_id=1, source_target_pairs={{0,4},{4,8},{8,12},{12,16},{16,20},{20,24},{24,28},{28,32},{32,36}... | collective-permute-start | bytes 122888 | tf_op jit(solution)/shard_map/ppermute | solution.py:23
  141.4 15.9 %collective-permute-start.5 = (f32[5,1,16,128]{3,2,1,0:T(8,128)S(1)}, f32[5,1,16,128]{3,2,1,0:T(8,128)S(1)}, u32[]{:S(2)}, u32[]{:S(2)}) collective-permute-start(f32[5,1,16,128]{3,2,1,0:T(8,128)S(1)} %get-tuple-element.373), channel_id=1, source_target_pairs={{4,0},{8,4},{12,8},{16,12},{20,16},{24,20},{28,24},{32,28},{36,32}... | collective-permute-start | bytes 122888 | tf_op jit(solution)/shard_map/ppermute | solution.py:24
  157.3 4.9 %collective-permute-start.6 = (f32[5,6,1,128]{3,2,1,0:T(1,128)S(1)}, f32[5,6,1,128]{3,2,1,0:T(1,128)S(1)}, u32[]{:S(2)}, u32[]{:S(2)}) collective-permute-start(f32[5,6,1,128]{3,2,1,0:T(1,128)S(1)} %get-tuple-element.368), channel_id=1, source_target_pairs={{0,1},{1,2},{2,3},{4,5},{5,6},{6,7},{8,9},{9,10},{10,11},{12,13},{... | collective-permute-start | bytes 46088 | tf_op jit(solution)/shard_map/ppermute | solution.py:23
  160.1 13.8 %collective-permute-start.7 = (f32[5,6,1,128]{3,2,1,0:T(1,128)S(1)}, f32[5,6,1,128]{3,2,1,0:T(1,128)S(1)}, u32[]{:S(2)}, u32[]{:S(2)}) collective-permute-start(f32[5,6,1,128]{3,2,1,0:T(1,128)S(1)} %get-tuple-element.369), channel_id=1, source_target_pairs={{1,0},{2,1},{3,2},{5,4},{6,5},{7,6},{9,8},{10,9},{11,10},{13,12},{... | collective-permute-start | bytes 46088 | tf_op jit(solution)/shard_map/ppermute | solution.py:24
where the time goes:
time: 368 us; the launch traced here: 367 us
  other arithmetic  158 us (43%)
  blocking collectives  104 us (28%)
  starting transfers between devices  57.6 us (16%)
  waiting for transfers between devices  25.5 us (7%)
  loops' own time  16.1 us (4%)
  local copies, waits for them, and re-layouts  5.42 us (1%)
    reduce_sum x32, other arithmetic, column_rates(): force_x = force_x + jnp.sum(pressure * delta_x, axis=2)  152 us
    pmin x1, blocking collectives, body(): lowest = lax.pmin(own_lowest, ('chan', 'cross'))  104 us
    ppermute x4, starting transfers between devices, padded_2(): after = lax.ppermute(leading, axis, down)  35 us
    ppermute x4, waiting for transfers between devices, padded_2(): after = lax.ppermute(leading, axis, down)  25.5 us
    ppermute x4, starting transfers between devices, padded_2(): before = lax.ppermute(last, axis, up)  22.5 us
    another operation x2, loops' own time, local_rates(): per_column = lax.map(one_column, columns)  16.1 us
  transfers between devices with their start and end apart: 8, of which 4 were waited for; matrix products, arithmetic and copies ran while one was open for 0% of the time, Pallas kernels for 0%

commit v1 on v0

v1 whole, which is shorter than its diff:
```python
import math

import jax
import jax.numpy as jnp
from jax import lax
from jax.experimental import pallas as pl
from jax.experimental.pallas import tpu as pltpu
from jax.sharding import PartitionSpec as P

SOUND_SQ = 100.0
KERNEL_GRAD = 140.0 / math.pi
PARTICLE_MASS = 1.0 / 128.0
GRAVITY = 1.0
TIME_STEP = 0.025
FORCE_SCALE = KERNEL_GRAD * PARTICLE_MASS
HALF = 0.5 * TIME_STEP

S = 128
NX = 4
NY = 16
HALO = 2
COLS = NX + 2 * HALO
SLOTS = NY + 2 * HALO + 4
BASE = HALO + 2
NB = COLS * SLOTS
GEO = 16
SUMF = 24
FEAT = GEO + SUMF
OFFSETS = ((0, 0), (0, 1), (1, -1), (1, 0), (1, 1))
FAR = 64.0


def split(x, pieces):
    out = []
    for _ in range(pieces - 1):
        h = x.astype(jnp.bfloat16).astype(jnp.float32)
        out.append(h)
        x = x - h
    out.append(x)
    return out


def grid_coords():
    row = lax.broadcasted_iota(jnp.int32, (NB, S), 0)
    col = (row * 171) >> 12
    slot = row - col * SLOTS
    cx = col.astype(jnp.float32) - 0.5 * (COLS - 1)
    cy = slot.astype(jnp.float32) - 0.5 * (SLOTS - 1)
    return cx, cy


def build(x, y, u, v, rho, occ, feat_ref, geo_ref, comb_ref, acc_ref):
    def put(ref, width, f, val):
        ref[pl.ds(f, NB, stride=width), :] = val

    zero = jnp.zeros((NB, S), jnp.float32)
    one = jnp.ones((NB, S), jnp.float32)
    off = (1.0 - occ) * FAR
    xs = split(x, 2)
    ys = split(y, 2)
    xt = xs[0] + xs[1].astype(jnp.bfloat16).astype(jnp.float32)
    yt = ys[0] + ys[1].astype(jnp.bfloat16).astype(jnp.float32)
    rr = split(xt * xt + yt * yt + off, 3)
    rows = [xs[0], xs[0], xs[1], xs[1], ys[0], ys[0], ys[1], ys[1], *rr, one, one, one]
    cx, cy = grid_coords()
    gx = cx + x
    gy = cy + y
    p = SOUND_SQ * (rho - 1.0) * occ
    rows += [zero, zero]
    rows += [one]
    rows += split(gx, 3) + split(gy, 3) + split(p, 2) + split(p * gx, 3) + split(p * gy, 3)
    rows += split(u, 2) + split(v, 2) + split(u * gx + v * gy, 3)
    rows += [zero] * (FEAT - len(rows))
    for f, val in enumerate(rows):
        put(feat_ref, FEAT, f, val)
    for k, (dx, dy) in enumerate(OFFSETS):
        bx = x + dx
        by = y + dy
        hx = split(bx, 2)
        hy = split(by, 2)
        tx = hx[0] + hx[1].astype(jnp.bfloat16).astype(jnp.float32)
        ty = hy[0] + hy[1].astype(jnp.bfloat16).astype(jnp.float32)
        nn = split(tx * tx + ty * ty + off, 3)
        g = [-2.0 * hx[0], -2.0 * hx[1], -2.0 * hx[0], -2.0 * hx[1]]
        g += [-2.0 * hy[0], -2.0 * hy[1], -2.0 * hy[0], -2.0 * hy[1]]
        g += [one, one, one, *nn, zero, zero]
        for f, val in enumerate(g):
            geo_ref[pl.ds(k * NB * GEO + f, NB, stride=GEO), :] = val

    def turn(r, carry):
        block = feat_ref[pl.ds(pl.multiple_of(r * FEAT, 8), FEAT), :]
        comb_ref[r] = block.T.astype(jnp.bfloat16)
        return carry

    lax.fori_loop(0, NB, turn, 0, unroll=4)
    acc_ref[...] = jnp.zeros_like(acc_ref)


def interact(a, ks, fine, feat_ref, geo_ref, comb_ref, acc_ref):
    bins = [a + OFFSETS[k][0] * SLOTS + OFFSETS[k][1] for k in ks]
    lhs = comb_ref[a][:, :GEO]
    g = jnp.concatenate(
        [geo_ref[pl.ds(pl.multiple_of((k * NB + b) * GEO, 8), GEO), :] for k, b in zip(ks, bins)], axis=1
    ).astype(jnp.bfloat16)
    r2 = jnp.dot(lhs, g, preferred_element_type=jnp.float32)
    t = jnp.maximum(r2, 1e-30)
    q = jnp.maximum(1.0 - t * lax.rsqrt(t), 0.0)
    w = q * q * q
    parts = [w.astype(jnp.bfloat16)]
    if fine:
        parts.append((w - parts[0].astype(jnp.float32)).astype(jnp.bfloat16))
    right = jnp.concatenate([comb_ref[b] for b in bins], axis=0)
    left = feat_ref[pl.ds(pl.multiple_of(a * FEAT + GEO, 8), SUMF), :].astype(jnp.bfloat16)
    to_a = sum(jnp.dot(w_, right, preferred_element_type=jnp.float32) for w_ in parts)
    to_b = sum(jnp.dot(left, w_, preferred_element_type=jnp.float32) for w_ in parts)
    at = pl.ds(pl.multiple_of(a * SUMF, 8), SUMF)
    acc_ref[at, :] = acc_ref[at, :] + to_a.T[GEO:FEAT]
    for n, (k, b) in enumerate(zip(ks, bins)):
        if k == 0:
            continue
        at = pl.ds(pl.multiple_of(b * SUMF, 8), SUMF)
        acc_ref[at, :] = acc_ref[at, :] + to_b[:, n * S : (n + 1) * S]


def sweep(ring, fine, refs):
    c0, c1 = ring + 1, COLS - 2 - ring
    s0, s1 = ring + 3, SLOTS - 4 - ring

    def column(c, carry):
        def row(s, carry):
            interact(c * SLOTS + s, (0, 1, 2, 3, 4), fine, *refs)
            return carry

        return lax.fori_loop(s0 - 1, s1 + 1, row, carry)

    lax.fori_loop(c0, c1 + 1, column, 0)

    def rim(t, carry):
        n = s1 - s0 + 3
        a = jnp.where(t < n, (c0 - 1) * SLOTS + s0 - 1 + t, (c0 + t - n) * SLOTS + s1 + 1)
        interact(a, (2, 3, 4), fine, *refs)
        return carry

    lax.fori_loop(0, s1 - s0 + 3 + c1 - c0, rim, 0)


def gather_rates(x, y, u, v, rho, occ, acc_ref):
    def get(f):
        return acc_ref[pl.ds(f, NB, stride=SUMF), :]

    cx, cy = grid_coords()
    gx = cx + x
    gy = cy + y
    p = SOUND_SQ * (rho - 1.0) * occ
    s1 = get(0)
    sx = get(1) + (get(2) + get(3))
    sy = get(4) + (get(5) + get(6))
    sp = get(7) + get(8)
    spx = get(9) + (get(10) + get(11))
    spy = get(12) + (get(13) + get(14))
    su = get(15) + get(16)
    sv = get(17) + get(18)
    se = get(19) + (get(20) + get(21))
    dx = gx * s1 - sx
    dy = gy * s1 - sy
    fx = p * dx + (gx * sp - spx)
    fy = p * dy + (gy * sp - spy)
    comp = u * dx + v * dy - (gx * su + gy * sv - se)
    return FORCE_SCALE * fx, FORCE_SCALE * fy - GRAVITY, -FORCE_SCALE * comp


def step_kernel(ext_ref, new_ref, low_ref, feat_ref, geo_ref, comb_ref, acc_ref):
    refs = (feat_ref, geo_ref, comb_ref, acc_ref)

    def load():
        rho = ext_ref[4]
        occ = jnp.where(rho > 0.0, 1.0, 0.0)
        x = (ext_ref[0] - 0.5) * occ
        y = (ext_ref[1] - 0.5) * occ
        return x, y, ext_ref[2] * occ, ext_ref[3] * occ, rho, occ

    x, y, u, v, rho, occ = load()
    build(x, y, u, v, rho, occ, *refs)
    sweep(0, False, refs)
    x, y, u, v, rho, occ = load()
    ax, ay, ar = gather_rates(x, y, u, v, rho, occ, acc_ref)

    def predicted():
        return (
            (x + HALF * u) * occ,
            (y + HALF * v) * occ,
            (u + HALF * ax) * occ,
            (v + HALF * ay) * occ,
            (rho + HALF * ar) * occ,
        )

    px, py, pu, pv, pr = predicted()
    build(px, py, pu, pv, pr, occ, *refs)
    sweep(1, True, refs)
    ax, ay, ar = gather_rates(px, py, pu, pv, pr, occ, acc_ref)
    x, y, u, v, rho, occ = load()
    nu = u + TIME_STEP * ax
    nv = v + TIME_STEP * ay
    nx = ext_ref[0] + HALF * (u + nu)
    ny = ext_ref[1] + HALF * (v + nv)
    nr = rho + TIME_STEP * ar
    low = jnp.where(occ > 0.0, nr, 1000000000.0)
    lows = []
    for c in range(NX):
        at = slice((c + HALO) * SLOTS + BASE, (c + HALO) * SLOTS + BASE + NY)
        for f, val in enumerate((nx, ny, nu, nv, nr)):
            new_ref[f, c] = jnp.where(occ[at] > 0.0, val[at], 0.0)
        lows.append(low[at])
    low_ref[...] = jnp.min(jnp.concatenate(lows, axis=0), axis=0, keepdims=True)


def sph_step(ext):
    return pl.pallas_call(
        step_kernel,
        out_shape=(
            jax.ShapeDtypeStruct((5, NX, NY, S), jnp.float32),
            jax.ShapeDtypeStruct((1, S), jnp.float32),
        ),
        in_specs=[pl.BlockSpec(memory_space=pltpu.VMEM)],
        out_specs=(
            pl.BlockSpec(memory_space=pltpu.VMEM),
            pl.BlockSpec(memory_space=pltpu.VMEM),
        ),
        scratch_shapes=[
            pltpu.VMEM((NB * FEAT, S), jnp.float32),
            pltpu.VMEM((len(OFFSETS) * NB * GEO, S), jnp.float32),
            pltpu.VMEM((NB, S, FEAT), jnp.bfloat16),
            pltpu.VMEM((NB * SUMF, S), jnp.float32),
        ],
        name="sph_step",
    )(ext)


def padded(x, axis, dim, width, wrap):
    size, length = lax.axis_size(axis), x.shape[dim]
    up = [(i, (i + 1) % size) for i in range(size if wrap else size - 1)]
    down = [(j, i) for i, j in up]
    last = lax.slice_in_dim(x, length - width, length, axis=dim)
    leading = lax.slice_in_dim(x, 0, width, axis=dim)
    before = lax.ppermute(last, axis, up)
    after = lax.ppermute(leading, axis, down)
    return jnp.concatenate([before, x, after], axis=dim)


def body(positions, velocity, density, counts):
    slot_index = jnp.arange(S, dtype=jnp.int32)
    rho = jnp.where(slot_index[None, None, :] < counts[:, :, None], density, 0.0)
    fields = jnp.concatenate([positions, velocity, rho[None]], axis=0)
    ext = padded(fields, "chan", 1, HALO, True)
    ext = padded(ext, "cross", 2, HALO, False)
    ext = jnp.pad(ext, ((0, 0), (0, 0), (BASE - HALO, SLOTS - NY - HALO - BASE), (0, 0)))
    new_fields, low = sph_step(ext.reshape(5, NB, S))
    own = jnp.broadcast_to(jnp.min(low), (lax.axis_size("chan") * lax.axis_size("cross"), S))
    everyone = lax.all_to_all(own, ("chan", "cross"), 0, 0, tiled=True)
    return (new_fields, jnp.min(everyone))


def solution(mesh):
    return jax.shard_map(
        body,
        mesh=mesh,
        in_specs=(
            P(None, "chan", "cross", None),
            P(None, "chan", "cross", None),
            P("chan", "cross", None),
            P("chan", "cross"),
        ),
        out_specs=(P(None, "chan", "cross", None), P()),
        check_vma=False,
    )
```

time: 368 us -> 221 us (0.60)
  other arithmetic: 158 us -> 3.95 us
  Pallas kernels: 0 us -> 123 us
  blocking collectives: 104 us -> 41.8 us
  starting transfers between devices: 57.6 us -> 36 us
  loops' own time: 16.1 us -> 0 us
  waiting for transfers between devices: 25.5 us -> 13.6 us
  local copies, waits for them, and re-layouts: 5.42 us -> 1.46 us
    reduce_sum x32 -> x0, other arithmetic: 152 us -> none  [column_rates(): force_x = force_x + jnp.sum(pressure * delta_x, axis=2)]
    pallas_call x0 -> x1, Pallas kernels: none -> 123 us  [sph_step(): pl.pallas_call(step_kernel, out_shape=(jax.ShapeDtypeStruct((5, NX, NY, S...]
    pmin x1 -> x0, blocking collectives: 104 us -> none  [body(): lowest = lax.pmin(own_lowest, ('chan', 'cross'))]
    all_to_all x0 -> x1, blocking collectives: none -> 41.8 us  [body(): everyone = lax.all_to_all(own, ('chan', 'cross'), 0, 0, tiled=True)]
    ppermute x8 -> x4, starting transfers between devices: 57.6 us -> 36 us  [the longest x2 18.2 us: padded(): after = lax.ppermute(leading, axis, down)]
    another operation x2 -> x0, loops' own time: 16.1 us -> none  [local_rates(): per_column = lax.map(one_column, columns)]
    ppermute x8 -> x4, waiting for transfers between devices: 25.5 us -> 13.6 us  [the longest x2 13.5 us: padded(): after = lax.ppermute(leading, axis, down)]
    dynamic_slice x8 -> x0, local copies, waits for them, and re-layouts: 4.7 us -> none  [local_rates(): per_column = lax.map(one_column, columns)]
  transfers between devices with their start and end apart: 8 -> 4, of which waited for: 4 -> 2; matrix products, arithmetic and copies ran while one was open for 0% -> 0% of each run, Pallas kernels for 0% -> 0%
where the time goes in v1:
time: 221 us
  Pallas kernels  123 us (56%)
  blocking collectives  41.8 us (19%)
  starting transfers between devices  36 us (16%)
  waiting for transfers between devices  13.6 us (6%)
  other arithmetic  3.95 us (2%)
    pallas_call x1, Pallas kernels, sph_step(): pl.pallas_call(step_kernel, out_shape=(jax.ShapeDtypeStruct((5, NX, NY, S...  123 us
    all_to_all x1, blocking collectives, body(): everyone = lax.all_to_all(own, ('chan', 'cross'), 0, 0, tiled=True)  41.8 us
    ppermute x2, starting transfers between devices, padded(): after = lax.ppermute(leading, axis, down)  18.2 us
    ppermute x2, starting transfers between devices, padded(): before = lax.ppermute(last, axis, up)  17.8 us
    ppermute x2, waiting for transfers between devices, padded(): after = lax.ppermute(leading, axis, down)  13.5 us
  transfers between devices with their start and end apart: 4, of which 2 were waited for; matrix products, arithmetic and copies ran while one was open for 0% of the time, Pallas kernels for 0%

profile of v1, /device:TPU:1, one launch (start us, length us, event | category | flops | bytes accessed | tf_op | source)
XLA Modules:
  0.0 220.5 jit_solution(15203285195935920458)
XLA Ops:
  0.6 0.0 copy-start
  0.6 0.9 select_bitcast_fusion
  1.5 0.0 copy-done
  1.5 0.9 pad_maximum_fusion
  2.4 0.0 copy-start.1
  2.4 4.0 %collective-permute-start = (f32[5,2,16,128]{3,2,1,0:T(8,128)S(1)}, f32[5,2,16,128]{3,2,1,0:T(8,128)S(1)}, u32[]{:S(2)}, u32[]{:S(2)}) collective-permute-start(f32[5,2,16,128]{3,2,1,0:T(8,128)S(1)} %get-tuple-element.8), channel_id=1, source_target_pairs={{0,4},{4,8},{8,12},{12,16},{16,20},{20,24},{24,28},{28,32},{32,36}... | collective-permute-start | bytes 245768 | tf_op jit(solution)/shard_map/ppermute | solution.py:245
  6.4 16.2 %collective-permute-start.1 = (f32[5,2,16,128]{3,2,1,0:T(8,128)S(1)}, f32[5,2,16,128]{3,2,1,0:T(8,128)S(1)}, u32[]{:S(2)}, u32[]{:S(2)}) collective-permute-start(f32[5,2,16,128]{3,2,1,0:T(8,128)S(1)} %get-tuple-element.9), channel_id=1, source_target_pairs={{4,0},{8,4},{12,8},{16,12},{20,16},{24,20},{28,24},{32,28},{36,32}... | collective-permute-start | bytes 245768 | tf_op jit(solution)/shard_map/ppermute | solution.py:246
  22.7 0.0 collective-permute-done
  22.7 1.5 collective-permute-done.1
  24.1 0.0 copy-done.1
  24.2 13.8 %collective-permute-start.2 = (f32[5,8,2,128]{3,2,1,0:T(2,128)S(1)}, f32[5,8,2,128]{3,2,1,0:T(2,128)S(1)}, u32[]{:S(2)}, u32[]{:S(2)}) collective-permute-start(f32[5,8,2,128]{3,2,1,0:T(2,128)S(1)} %get-tuple-element.6), channel_id=1, source_target_pairs={{0,1},{1,2},{2,3},{4,5},{5,6},{6,7},{8,9},{9,10},{10,11},{12,13},{... | collective-permute-start | bytes 122888 | tf_op jit(solution)/shard_map/ppermute | solution.py:245
  38.0 1.9 collective-permute-start.3
  39.9 0.0 collective-permute-done.2
  39.9 12.1 %collective-permute-done.3 = f32[5,8,2,128]{3,2,1,0:T(2,128)S(1)} collective-permute-done((f32[5,8,2,128]{3,2,1,0:T(2,128)S(1)}, f32[5,8,2,128]{3,2,1,0:T(2,128)S(1)}, u32[]{:S(2)}, u32[]{:S(2)}) %collective-permute-start.3) | collective-permute-done | bytes 40992 | tf_op jit(solution)/shard_map/ppermute | solution.py:246
  52.0 0.9 select_maximum_fusion
  53.0 123.0 %sph_step.1 = (f32[5,4,16,128]{3,2,1,0:T(8,128)}, f32[1,128]{1,0:T(1,128)}) custom-call(f32[5,192,128]{2,1,0:T(8,128)} %bitcast.4), custom_call_target="tpu_custom_call" | custom-call | tf_op jit(solution)/shard_map/sph_step/pallas_call | solution.py:218
  176.0 0.0 copy-start.2
  176.0 0.7 copy-done.2
  176.6 0.6 reduce_min.18
  177.2 0.8 broadcast_in_dim.14
  178.0 41.8 %all_to_all.6 = f32[512,1,128]{2,1,0:T(1,128)S(1)} all-to-all(f32[512,1,128]{2,1,0:T(1,128)S(1)} %broadcast_in_dim.14), channel_id=1, replica_groups=mesh['chan'=128,'cross'=4] {'chan','cross'}, dimensions={0} | all-to-all | bytes 524288 | tf_op jit(solution)/shard_map/all_to_all | solution.py:259
  219.8 0.7 reduce_min.19
  (2 shorter events, 0.0 us)
Async XLA Ops:
  0.6 0.9 copy-start
  2.4 21.8 %copy-start.1 = (f32[2,4,16,128]{3,2,1,0:T(8,128)S(1)}, f32[2,4,16,128]{3,2,1,0:T(8,128)}, u32[]{:S(2)}) copy-start(f32[2,4,16,128]{3,2,1,0:T(8,128)} %param.4) | copy-start | bytes 196612
  2.4 20.3 %collective-permute-start = (f32[5,2,16,128]{3,2,1,0:T(8,128)S(1)}, f32[5,2,16,128]{3,2,1,0:T(8,128)S(1)}, u32[]{:S(2)}, u32[]{:S(2)}) collective-permute-start(f32[5,2,16,128]{3,2,1,0:T(8,128)S(1)} %get-tuple-element.8), channel_id=1, source_target_pairs={{0,4},{4,8},{8,12},{12,16},{16,20},{20,24},{24,28},{28,32},{32,36}... | collective-permute-start | bytes 245768 | tf_op jit(solution)/shard_map/ppermute | solution.py:245
  6.4 17.7 %collective-permute-start.1 = (f32[5,2,16,128]{3,2,1,0:T(8,128)S(1)}, f32[5,2,16,128]{3,2,1,0:T(8,128)S(1)}, u32[]{:S(2)}, u32[]{:S(2)}) collective-permute-start(f32[5,2,16,128]{3,2,1,0:T(8,128)S(1)} %get-tuple-element.9), channel_id=1, source_target_pairs={{4,0},{8,4},{12,8},{16,12},{20,16},{24,20},{28,24},{32,28},{36,32}... | collective-permute-start | bytes 245768 | tf_op jit(solution)/shard_map/ppermute | solution.py:246
  24.2 15.7 %collective-permute-start.2 = (f32[5,8,2,128]{3,2,1,0:T(2,128)S(1)}, f32[5,8,2,128]{3,2,1,0:T(2,128)S(1)}, u32[]{:S(2)}, u32[]{:S(2)}) collective-permute-start(f32[5,8,2,128]{3,2,1,0:T(2,128)S(1)} %get-tuple-element.6), channel_id=1, source_target_pairs={{0,1},{1,2},{2,3},{4,5},{5,6},{6,7},{8,9},{9,10},{10,11},{12,13},{... | collective-permute-start | bytes 122888 | tf_op jit(solution)/shard_map/ppermute | solution.py:245
  38.0 14.0 %collective-permute-start.3 = (f32[5,8,2,128]{3,2,1,0:T(2,128)S(1)}, f32[5,8,2,128]{3,2,1,0:T(2,128)S(1)}, u32[]{:S(2)}, u32[]{:S(2)}) collective-permute-start(f32[5,8,2,128]{3,2,1,0:T(2,128)S(1)} %get-tuple-element.7), channel_id=1, source_target_pairs={{1,0},{2,1},{3,2},{5,4},{6,5},{7,6},{9,8},{10,9},{11,10},{13,12},{... | collective-permute-start | bytes 122888 | tf_op jit(solution)/shard_map/ppermute | solution.py:246
  176.0 0.7 copy-start.2

commit v2 on v1

v2 whole, which is shorter than its diff:
```python
import math

import jax
import jax.numpy as jnp
from jax import lax
from jax.experimental import pallas as pl
from jax.experimental.pallas import tpu as pltpu
from jax.sharding import PartitionSpec as P

SOUND_SQ = 100.0
KERNEL_GRAD = 140.0 / math.pi
PARTICLE_MASS = 1.0 / 128.0
GRAVITY = 1.0
TIME_STEP = 0.025
FORCE_SCALE = KERNEL_GRAD * PARTICLE_MASS
HALF = 0.5 * TIME_STEP

S = 128
NX = 4
NY = 16
HALO = 2
COLS = NX + 2 * HALO
SLOTS = NY + 2 * HALO + 4
BASE = HALO + 2
NB = COLS * SLOTS
SUMF = 24
TALL = 32
OFFSETS = ((0, 0), (0, 1), (1, -1), (1, 0), (1, 1))
FAR = 1000.0
PLANE = 32


def split(x, pieces):
    out = []
    for _ in range(pieces - 1):
        h = x.astype(jnp.bfloat16).astype(jnp.float32)
        out.append(h)
        x = x - h
    out.append(x)
    return out


def on_grid(x, y):
    row = lax.broadcasted_iota(jnp.int32, (NB, S), 0)
    col = (row * 171) >> 12
    slot = row - col * SLOTS
    return (
        x + (col.astype(jnp.float32) - 0.5 * (COLS - 1)),
        y + (slot.astype(jnp.float32) - 0.5 * (SLOTS - 1)),
    )


def build(x, y, u, v, rho, occ, direct, refs):
    plane_ref, turned_ref, gx_ref, gy_ref, p_ref, u_ref, v_ref, acc_ref = refs
    acc_ref[...] = jnp.zeros_like(acc_ref)
    gx, gy = on_grid(x, y)
    gx_ref[...] = jnp.where(occ > 0.0, gx, FAR)
    gy_ref[...] = gy
    p = SOUND_SQ * (rho - 1.0) * occ
    if direct:
        p_ref[...] = p
        u_ref[...] = u
        v_ref[...] = v
        return
    gx = gx * occ
    gy = gy * occ
    rows = [occ] + split(gx, 3) + split(gy, 3) + split(u, 2) + split(v, 2) + split(u * gx + v * gy, 3)
    rows += split(p, 2) + split(p * gx, 3) + split(p * gy, 3)
    rows += [jnp.zeros((NB, S), jnp.float32)] * (SUMF - len(rows))
    for f, val in enumerate(rows):
        plane_ref[f * NB : (f + 1) * NB, :] = val

    def turn(r, carry):
        block = plane_ref[pl.ds(r, SUMF, stride=NB), :]
        block = jnp.concatenate([block, jnp.zeros((TALL - SUMF, S), jnp.float32)], axis=0)
        turned_ref[r] = block.astype(jnp.bfloat16)
        return carry

    lax.fori_loop(0, NB, turn, 0, unroll=8)


def geometry(a, bins, refs):
    gx_ref, gy_ref = refs[2], refs[3]
    ax = down(gx_ref, a)
    ay = down(gy_ref, a)
    for b in bins:
        dx = ax - gx_ref[pl.ds(b, 1), :]
        dy = ay - gy_ref[pl.ds(b, 1), :]
        t = jnp.maximum(dx * dx + dy * dy, 1e-30)
        q = jnp.maximum(1.0 - t * lax.rsqrt(t), 0.0)
        yield b, dx, dy, q * q * q


def down(ref, a):
    return jnp.broadcast_to(ref[pl.ds(a, 1), :], (S, S)).T


def pair_sums(a, ks, direct, refs):
    bins = [a + OFFSETS[k][0] * SLOTS + OFFSETS[k][1] for k in ks]
    if direct:
        return direct_sums(a, bins, ks, refs)
    turned_ref = refs[1]
    w = jnp.concatenate([w.astype(jnp.bfloat16) for _, _, _, w in geometry(a, bins, refs)], axis=1)
    right = jnp.concatenate([turned_ref[b] for b in bins], axis=1)
    to_a = lax.dot_general(right, w, (((1,), (1,)), ((), ())), preferred_element_type=jnp.float32)
    to_b = jnp.dot(turned_ref[a], w, preferred_element_type=jnp.float32)
    out = [(a, to_a[:SUMF])]
    for n, (k, b) in enumerate(zip(ks, bins)):
        if k != 0:
            out.append((b, to_b[:SUMF, n * S : (n + 1) * S]))
    return out


def direct_sums(a, bins, ks, refs):
    p_ref, u_ref, v_ref = refs[4:7]
    ap, au, av = (down(ref, a) for ref in (p_ref, u_ref, v_ref))
    rows = None
    out = []
    fill = jnp.zeros((8 - 3, S), jnp.float32)
    for k, (b, dx, dy, w) in zip(ks, geometry(a, bins, refs)):
        at = pl.ds(b, 1)
        wx = w * dx
        wy = w * dy
        p = ap + p_ref[at, :]
        vals = (p * wx, p * wy, (au - u_ref[at, :]) * wx + (av - v_ref[at, :]) * wy)
        rows = vals if rows is None else tuple(r + x for r, x in zip(rows, vals))
        if k != 0:
            fx, fy, co = (jnp.sum(x, axis=0, keepdims=True) for x in vals)
            out.append((b, jnp.concatenate([-fx, -fy, co, fill], axis=0)))
    rows = [jnp.sum(r.T, axis=0, keepdims=True) for r in rows]
    out.append((a, jnp.concatenate([*rows, fill], axis=0)))
    return out


def interact(many, ks, direct, refs):
    acc_ref = refs[-1]
    sums = [pair_sums(a, ks, direct, refs) for a in many]
    for group in sums:
        for b, val in group:
            at = pl.ds(pl.multiple_of(b * SUMF, 8), val.shape[0])
            acc_ref[at, :] = acc_ref[at, :] + val


def sweep(ring, direct, many, refs):
    c0, c1 = ring + 1, COLS - 2 - ring
    s0, s1 = ring + 3, SLOTS - 4 - ring
    step = (c1 - c0 + 1) // many

    def column(c, carry):
        def row(s, carry):
            interact([(c + step * m) * SLOTS + s for m in range(many)], (0, 1, 2, 3, 4), direct, refs)
            return carry

        return lax.fori_loop(s0 - 1, s1 + 1, row, carry)

    lax.fori_loop(c0, c0 + step, column, 0)
    n = s1 - s0 + 3
    total = n + c1 - c0
    group = 5 if total % 5 == 0 else 3 if total % 3 == 0 else 1

    def rim(i, carry):
        ts = [i * group + m for m in range(group)]
        at = [jnp.where(t < n, (c0 - 1) * SLOTS + s0 - 1 + t, (c0 + t - n) * SLOTS + s1 + 1) for t in ts]
        interact(at, (2, 3, 4), direct, refs)
        return carry

    lax.fori_loop(0, total // group, rim, 0)


def gather_rates(x, y, u, v, rho, occ, direct, acc_ref):
    def get(f):
        return acc_ref[pl.ds(f, NB, stride=SUMF), :]

    if direct:
        fx, fy, comp = get(0), get(1), get(2)
    else:
        gx, gy = on_grid(x, y)
        s1 = get(0)
        dx = gx * s1 - (get(1) + (get(2) + get(3)))
        dy = gy * s1 - (get(4) + (get(5) + get(6)))
        se = get(11) + (get(12) + get(13))
        comp = u * dx + v * dy - (gx * (get(7) + get(8)) + gy * (get(9) + get(10)) - se)
        p = SOUND_SQ * (rho - 1.0) * occ
        sp = get(14) + get(15)
        fx = p * dx + (gx * sp - (get(16) + (get(17) + get(18))))
        fy = p * dy + (gy * sp - (get(19) + (get(20) + get(21))))
    return FORCE_SCALE * fx, FORCE_SCALE * fy - GRAVITY, -FORCE_SCALE * comp


def step_kernel(ext_ref, new_ref, low_ref, *refs):
    acc_ref = refs[-1]

    def load():
        rho = ext_ref[4]
        occ = jnp.where(rho > 0.0, 1.0, 0.0)
        x = (ext_ref[0] - 0.5) * occ
        y = (ext_ref[1] - 0.5) * occ
        return x, y, ext_ref[2] * occ, ext_ref[3] * occ, rho, occ

    x, y, u, v, rho, occ = load()
    build(x, y, u, v, rho, occ, False, refs)
    sweep(0, False, 3, refs)
    x, y, u, v, rho, occ = load()
    ax, ay, ar = gather_rates(x, y, u, v, rho, occ, False, acc_ref)

    def predicted():
        return (
            (x + HALF * u) * occ,
            (y + HALF * v) * occ,
            (u + HALF * ax) * occ,
            (v + HALF * ay) * occ,
            (rho + HALF * ar) * occ,
        )

    px, py, pu, pv, pr = predicted()
    build(px, py, pu, pv, pr, occ, True, refs)
    sweep(1, True, 2, refs)
    ax, ay, ar = gather_rates(px, py, pu, pv, pr, occ, True, acc_ref)
    x, y, u, v, rho, occ = load()
    nu = u + TIME_STEP * ax
    nv = v + TIME_STEP * ay
    nx = ext_ref[0] + HALF * (u + nu)
    ny = ext_ref[1] + HALF * (v + nv)
    nr = rho + TIME_STEP * ar
    low = jnp.where(occ > 0.0, nr, 1000000000.0)
    lows = []
    for c in range(NX):
        at = slice((c + HALO) * SLOTS + BASE, (c + HALO) * SLOTS + BASE + NY)
        for f, val in enumerate((nx, ny, nu, nv, nr)):
            new_ref[f, c] = jnp.where(occ[at] > 0.0, val[at], 0.0)
        lows.append(low[at])
    low_ref[...] = jnp.broadcast_to(jnp.min(jnp.concatenate(lows, axis=0)), low_ref.shape)


def sph_step(ext):
    return pl.pallas_call(
        step_kernel,
        out_shape=(
            jax.ShapeDtypeStruct((5, NX, NY, S), jnp.float32),
            jax.ShapeDtypeStruct((PLANE, S), jnp.float32),
        ),
        in_specs=[pl.BlockSpec(memory_space=pltpu.VMEM)],
        out_specs=(
            pl.BlockSpec(memory_space=pltpu.VMEM),
            pl.BlockSpec(memory_space=pltpu.VMEM),
        ),
        scratch_shapes=[
            pltpu.VMEM((SUMF * NB, S), jnp.float32),
            pltpu.VMEM((NB, TALL, S), jnp.bfloat16),
            pltpu.VMEM((NB, S), jnp.float32),
            pltpu.VMEM((NB, S), jnp.float32),
            pltpu.VMEM((NB, S), jnp.float32),
            pltpu.VMEM((NB, S), jnp.float32),
            pltpu.VMEM((NB, S), jnp.float32),
            pltpu.VMEM((NB * SUMF, S), jnp.float32),
        ],
        name="sph_step",
    )(ext)


def swap(x, dim, axis, wrap):
    size, length = lax.axis_size(axis), x.shape[dim]
    even = lax.axis_index(axis) % 2 == 0
    last = lax.slice_in_dim(x, length - HALO, length, axis=dim)
    first = lax.slice_in_dim(x, 0, HALO, axis=dim)

    def pairs(start):
        ends = [(i, (i + 1) % size) for i in range(start, size if wrap else size - 1, 2)]
        return ends + [(j, i) for i, j in ends]

    near = lax.ppermute(jnp.where(even, last, first), axis, pairs(0))
    far = lax.ppermute(jnp.where(even, first, last), axis, pairs(1))
    return jnp.where(even, far, near), jnp.where(even, near, far)


def minimum_everywhere(low):
    chan, cross = lax.axis_size("chan"), lax.axis_size("cross")
    planes = {}
    for i in range(chan * cross):
        planes.setdefault((i // cross // 4 % 8, i % cross // 2), []).append(i)
    planes = list(planes.values())
    lines = [list(line) for line in zip(*planes)]
    both = ("chan", "cross")
    got = lax.all_to_all(low, both, 0, 0, tiled=True, axis_index_groups=planes)
    got = jnp.broadcast_to(jnp.min(got, axis=0, keepdims=True), (len(planes), S))
    return jnp.min(lax.all_to_all(got, both, 0, 0, tiled=True, axis_index_groups=lines))


def body(positions, velocity, density, counts):
    slot_index = jnp.arange(S, dtype=jnp.int32)
    rho = jnp.where(slot_index[None, None, :] < counts[:, :, None], density, 0.0)
    fields = jnp.concatenate([positions, velocity, rho[None]], axis=0)
    before, after = swap(fields, 1, "chan", True)
    wide = jnp.concatenate([before, fields, after], axis=1)
    below, above = swap(wide, 2, "cross", False)
    ext = jnp.concatenate([below, wide, above], axis=2)
    ext = jnp.pad(ext, ((0, 0), (0, 0), (BASE - HALO, SLOTS - NY - HALO - BASE), (0, 0)))
    new_fields, low = sph_step(ext.reshape(5, NB, S))
    return (new_fields, minimum_everywhere(low))


def solution(mesh):
    return jax.shard_map(
        body,
        mesh=mesh,
        in_specs=(
            P(None, "chan", "cross", None),
            P(None, "chan", "cross", None),
            P("chan", "cross", None),
            P("chan", "cross"),
        ),
        out_specs=(P(None, "chan", "cross", None), P()),
        check_vma=False,
    )
```

time: 221 us -> 146 us (0.66)
  Pallas kernels: 123 us -> 69.6 us
  blocking collectives: 41.8 us -> 30.2 us
  waiting for transfers between devices: 13.6 us -> 8.95 us
  starting transfers between devices: 36 us -> 32.6 us
    pallas_call x1, Pallas kernels: 123 us -> 69.6 us  [sph_step(): pl.pallas_call(step_kernel, out_shape=(jax.ShapeDtypeStruct((5, NX, NY, S...]
    all_to_all x1 -> x2, blocking collectives: 41.8 us -> 30.2 us  [the longest x1 20.4 us: minimum_everywhere(): lax.all_to_all(got, both, 0, 0, tiled=True, axis_index_groups=lines)]
    ppermute x4, waiting for transfers between devices: 13.6 us -> 8.95 us  [the longest x2 5.66 us: swap(): far = lax.ppermute(jnp.where(even, first, last), axis, pairs(1))]
    ppermute x4, starting transfers between devices: 36 us -> 32.6 us  [the longest x2 26.7 us: swap(): far = lax.ppermute(jnp.where(even, first, last), axis, pairs(1))]
where the time goes in v2:
time: 146 us; the launch traced here: 145 us
  Pallas kernels  69.6 us (48%)
  starting transfers between devices  32.6 us (22%)
  blocking collectives  30.2 us (21%)
  waiting for transfers between devices  8.95 us (6%)
  other arithmetic  3.39 us (2%)
    pallas_call x1, Pallas kernels, sph_step(): pl.pallas_call(step_kernel, out_shape=(jax.ShapeDtypeStruct((5, NX, NY, S...  69.6 us
    ppermute x2, starting transfers between devices, swap(): far = lax.ppermute(jnp.where(even, first, last), axis, pairs(1))  26.7 us
    all_to_all x1, blocking collectives, minimum_everywhere(): lax.all_to_all(got, both, 0, 0, tiled=True, axis_index_groups=lines)  20.4 us
    all_to_all x1, blocking collectives, minimum_everywhere(): got = lax.all_to_all(low, both, 0, 0, tiled=True, axis_index_groups=planes)  9.77 us
    ppermute x2, starting transfers between devices, swap(): near = lax.ppermute(jnp.where(even, last, first), axis, pairs(0))  5.87 us
    ppermute x2, waiting for transfers between devices, swap(): far = lax.ppermute(jnp.where(even, first, last), axis, pairs(1))  5.66 us
    ppermute x2, waiting for transfers between devices, swap(): near = lax.ppermute(jnp.where(even, last, first), axis, pairs(0))  3.29 us
  transfers between devices with their start and end apart: 4, of which 2 were waited for; matrix products, arithmetic and copies ran while one was open for 0% of the time, Pallas kernels for 0%

profile of v2, /device:TPU:1, one launch (start us, length us, event | category | flops | bytes accessed | tf_op | source)
XLA Modules:
  0.0 145.4 jit_solution(5214269294734207732)
XLA Ops:
  0.6 0.0 copy-start
  0.7 0.9 select_bitcast_fusion
  1.5 0.0 copy-done
  1.5 0.9 pad_maximum_fusion
  2.4 18.3 %collective-permute-start = (f32[5,2,16,128]{3,2,1,0:T(8,128)S(1)}, f32[5,2,16,128]{3,2,1,0:T(8,128)S(1)}, u32[]{:S(2)}, u32[]{:S(2)}) collective-permute-start(f32[5,2,16,128]{3,2,1,0:T(8,128)S(1)} %get-tuple-element.11), channel_id=1, source_target_pairs={{4,8},{12,16},{20,24},{28,32},{36,40},{44,48},{52,56},{60,64},{68,... | collective-permute-start | bytes 245768 | tf_op jit(solution)/shard_map/ppermute | solution.py:272
  20.8 1.9 %collective-permute-start.1 = (f32[5,2,16,128]{3,2,1,0:T(8,128)S(1)}, f32[5,2,16,128]{3,2,1,0:T(8,128)S(1)}, u32[]{:S(2)}, u32[]{:S(2)}) collective-permute-start(f32[5,2,16,128]{3,2,1,0:T(8,128)S(1)} %get-tuple-element.12), channel_id=1, source_target_pairs={{0,4},{8,12},{16,20},{24,28},{32,36},{40,44},{48,52},{56,60},{64,6... | collective-permute-start | bytes 245768 | tf_op jit(solution)/shard_map/ppermute | solution.py:271
  22.7 0.0 copy-start.1
  22.7 0.0 collective-permute-done
  22.7 3.3 %collective-permute-done.1 = f32[5,2,16,128]{3,2,1,0:T(8,128)S(1)} collective-permute-done((f32[5,2,16,128]{3,2,1,0:T(8,128)S(1)}, f32[5,2,16,128]{3,2,1,0:T(8,128)S(1)}, u32[]{:S(2)}, u32[]{:S(2)}) %collective-permute-start.1) | collective-permute-done | bytes 81952 | tf_op jit(solution)/shard_map/ppermute | solution.py:271
  26.0 0.0 copy-done.1
  26.1 3.9 %collective-permute-start.3 = (f32[5,8,2,128]{3,2,1,0:T(2,128)S(1)}, f32[5,8,2,128]{3,2,1,0:T(2,128)S(1)}, u32[]{:S(2)}, u32[]{:S(2)}) collective-permute-start(f32[5,8,2,128]{3,2,1,0:T(2,128)S(1)} %bitcast.21), channel_id=1, source_target_pairs={{0,1},{2,3},{1,0},{3,2},{4,5},{6,7},{5,4},{7,6},{8,9},{10,11},{9,8... | collective-permute-start | bytes 122888 | tf_op jit(solution)/shard_map/ppermute | solution.py:271
  30.1 8.4 %collective-permute-start.2 = (f32[5,8,2,128]{3,2,1,0:T(2,128)S(1)}, f32[5,8,2,128]{3,2,1,0:T(2,128)S(1)}, u32[]{:S(2)}, u32[]{:S(2)}) collective-permute-start(f32[5,8,2,128]{3,2,1,0:T(2,128)S(1)} %get-tuple-element.6), channel_id=1, source_target_pairs={{1,2},{2,1},{5,6},{6,5},{9,10},{10,9},{13,14},{14,13},{17,18},{18,... | collective-permute-start | bytes 122888 | tf_op jit(solution)/shard_map/ppermute | solution.py:272
  38.4 0.0 collective-permute-done.3
  38.4 5.7 %collective-permute-done.2 = f32[5,8,2,128]{3,2,1,0:T(2,128)S(1)} collective-permute-done((f32[5,8,2,128]{3,2,1,0:T(2,128)S(1)}, f32[5,8,2,128]{3,2,1,0:T(2,128)S(1)}, u32[]{:S(2)}, u32[]{:S(2)}) %collective-permute-start.2) | collective-permute-done | bytes 40992 | tf_op jit(solution)/shard_map/ppermute | solution.py:272
  44.1 0.9 select_maximum_fusion
  45.0 69.6 %sph_step.1 = (f32[5,4,16,128]{3,2,1,0:T(8,128)}, f32[32,128]{1,0:T(8,128)}) custom-call(f32[5,192,128]{2,1,0:T(8,128)} %bitcast.14), custom_call_target="tpu_custom_call" | custom-call | tf_op jit(solution)/shard_map/sph_step/pallas_call | solution.py:236
  114.6 9.8 %all_to_all.15 = f32[32,1,128]{2,1,0:T(1,128)S(1)} all-to-all(f32[32,1,128]{2,1,0:T(1,128)} %bitcast.23), channel_id=1, replica_groups={{0,1,4,5,8,9,12,13,128,129,132,133,136,137,140,141,256,257,260,261,264,..., dimensions={0} | all-to-all | bytes 32768 | tf_op jit(solution)/shard_map/all_to_all | solution.py:284
  124.4 0.1 reduce_min.18
  124.4 20.4 %all_to_all.16 = f32[16,1,128]{2,1,0:T(1,128)S(1)} all-to-all(f32[16,1,128]{2,1,0:T(1,128)S(1)} %broadcast_in_dim.17), channel_id=1, replica_groups={{0,2,16,18,32,34,48,50,64,66,80,82,96,98,112,114},{1,3,17,19,33,35,49,5..., dimensions={0} | all-to-all | bytes 16384 | tf_op jit(solution)/shard_map/all_to_all | solution.py:286
  144.8 0.6 reduce_min.19
  (6 shorter events, 0.1 us)
Async XLA Ops:
  0.6 0.9 copy-start
  2.4 20.3 %collective-permute-start = (f32[5,2,16,128]{3,2,1,0:T(8,128)S(1)}, f32[5,2,16,128]{3,2,1,0:T(8,128)S(1)}, u32[]{:S(2)}, u32[]{:S(2)}) collective-permute-start(f32[5,2,16,128]{3,2,1,0:T(8,128)S(1)} %get-tuple-element.11), channel_id=1, source_target_pairs={{4,8},{12,16},{20,24},{28,32},{36,40},{44,48},{52,56},{60,64},{68,... | collective-permute-start | bytes 245768 | tf_op jit(solution)/shard_map/ppermute | solution.py:272
  20.8 5.3 %collective-permute-start.1 = (f32[5,2,16,128]{3,2,1,0:T(8,128)S(1)}, f32[5,2,16,128]{3,2,1,0:T(8,128)S(1)}, u32[]{:S(2)}, u32[]{:S(2)}) collective-permute-start(f32[5,2,16,128]{3,2,1,0:T(8,128)S(1)} %get-tuple-element.12), channel_id=1, source_target_pairs={{0,4},{8,12},{16,20},{24,28},{32,36},{40,44},{48,52},{56,60},{64,6... | collective-permute-start | bytes 245768 | tf_op jit(solution)/shard_map/ppermute | solution.py:271
  22.7 3.3 %copy-start.1 = (f32[2,4,16,128]{3,2,1,0:T(8,128)S(1)}, f32[2,4,16,128]{3,2,1,0:T(8,128)}, u32[]{:S(2)}) copy-start(f32[2,4,16,128]{3,2,1,0:T(8,128)} %param.4) | copy-start | bytes 196612
  26.1 12.3 %collective-permute-start.3 = (f32[5,8,2,128]{3,2,1,0:T(2,128)S(1)}, f32[5,8,2,128]{3,2,1,0:T(2,128)S(1)}, u32[]{:S(2)}, u32[]{:S(2)}) collective-permute-start(f32[5,8,2,128]{3,2,1,0:T(2,128)S(1)} %bitcast.21), channel_id=1, source_target_pairs={{0,1},{2,3},{1,0},{3,2},{4,5},{6,7},{5,4},{7,6},{8,9},{10,11},{9,8... | collective-permute-start | bytes 122888 | tf_op jit(solution)/shard_map/ppermute | solution.py:271
  30.1 14.0 %collective-permute-start.2 = (f32[5,8,2,128]{3,2,1,0:T(2,128)S(1)}, f32[5,8,2,128]{3,2,1,0:T(2,128)S(1)}, u32[]{:S(2)}, u32[]{:S(2)}) collective-permute-start(f32[5,8,2,128]{3,2,1,0:T(2,128)S(1)} %get-tuple-element.6), channel_id=1, source_target_pairs={{1,2},{2,1},{5,6},{6,5},{9,10},{10,9},{13,14},{14,13},{17,18},{18,... | collective-permute-start | bytes 122888 | tf_op jit(solution)/shard_map/ppermute | solution.py:272

commit v3 on v2

--- a/solution.py
+++ b/solution.py
@@ -24,8 +24,11 @@
 BASE = HALO + 2
 NB = COLS * SLOTS
 SUMF = 24
+WIDTH = SUMF + 8
 TALL = 32
 OFFSETS = ((0, 0), (0, 1), (1, -1), (1, 0), (1, 1))
+DIRECT = (0, 1)
+CHAIN = 2
 FAR = 1000.0
 PLANE = 32
 
@@ -50,18 +53,16 @@
     )
 
 
-def build(x, y, u, v, rho, occ, direct, refs):
+def build(x, y, u, v, rho, occ, low, high, refs):
     plane_ref, turned_ref, gx_ref, gy_ref, p_ref, u_ref, v_ref, acc_ref = refs
     acc_ref[...] = jnp.zeros_like(acc_ref)
     gx, gy = on_grid(x, y)
     gx_ref[...] = jnp.where(occ > 0.0, gx, FAR)
     gy_ref[...] = gy
     p = SOUND_SQ * (rho - 1.0) * occ
-    if direct:
-        p_ref[...] = p
-        u_ref[...] = u
-        v_ref[...] = v
-        return
+    p_ref[...] = p
+    u_ref[...] = u
+    v_ref[...] = v
     gx = gx * occ
     gy = gy * occ
     rows = [occ] + split(gx, 3) + split(gy, 3) + split(u, 2) + split(v, 2) + split(u * gx + v * gy, 3)
@@ -76,7 +77,7 @@
         turned_ref[r] = block.astype(jnp.bfloat16)
         return carry
 
-    lax.fori_loop(0, NB, turn, 0, unroll=8)
+    lax.fori_loop(low, high, turn, 0, unroll=8)
 
 
 def geometry(a, bins, refs):
@@ -95,95 +96,127 @@
     return jnp.broadcast_to(ref[pl.ds(a, 1), :], (S, S)).T
 
 
-def pair_sums(a, ks, direct, refs):
-    bins = [a + OFFSETS[k][0] * SLOTS + OFFSETS[k][1] for k in ks]
-    if direct:
-        return direct_sums(a, bins, ks, refs)
+def column_sums(chain, ks, fine, refs):
     turned_ref = refs[1]
-    w = jnp.concatenate([w.astype(jnp.bfloat16) for _, _, _, w in geometry(a, bins, refs)], axis=1)
-    right = jnp.concatenate([turned_ref[b] for b in bins], axis=1)
-    to_a = lax.dot_general(right, w, (((1,), (1,)), ((), ())), preferred_element_type=jnp.float32)
-    to_b = jnp.dot(turned_ref[a], w, preferred_element_type=jnp.float32)
-    out = [(a, to_a[:SUMF])]
-    for n, (k, b) in enumerate(zip(ks, bins)):
-        if k != 0:
-            out.append((b, to_b[:SUMF, n * S : (n + 1) * S]))
+    direct = DIRECT if fine else ()
+    p_ref, u_ref, v_ref = refs[4:7]
+    out = []
+    tiles = []
+    for a in chain:
+        bins = [a + OFFSETS[k][0] * SLOTS + OFFSETS[k][1] for k in ks]
+        rows = []
+        mine = {}
+        for k, (b, dx, dy, w) in zip(ks, geometry(a, bins, refs)):
+            if k not in direct:
+                mine[k] = [w.astype(jnp.bfloat16)]
+                if fine:
+                    mine[k].append((w - mine[k][0].astype(jnp.float32)).astype(jnp.bfloat16))
+                continue
+            if not rows:
+                ap, au, av = (down(ref, a) for ref in (p_ref, u_ref, v_ref))
+            at = pl.ds(b, 1)
+            wx = w * dx
+            wy = w * dy
+            p = ap + p_ref[at, :]
+            vals = (p * wx, p * wy, (au - u_ref[at, :]) * wx + (av - v_ref[at, :]) * wy)
+            rows = [r + x for r, x in zip(rows, vals)] if rows else list(vals)
+            if k != 0:
+                fx, fy, co = (jnp.sum(x, axis=0, keepdims=True) for x in vals)
+                out.append((b * WIDTH + SUMF, fill_rows(-fx, -fy, co)))
+        if rows:
+            rows = [jnp.sum(r.T, axis=0, keepdims=True) for r in rows]
+            out.append((a * WIDTH + SUMF, fill_rows(*rows)))
+        tiles.append(mine)
+        others = [k for k in mine if k != 0]
+        to_b = sum(
+            jnp.dot(turned_ref[a], jnp.concatenate([mine[k][n] for k in others], axis=1), preferred_element_type=jnp.float32)
+            for n in range(2 if fine else 1)
+        )
+        for n, k in enumerate(others):
+            b = a + OFFSETS[k][0] * SLOTS + OFFSETS[k][1]
+            out.append((b * WIDTH, to_b[:SUMF, n * S : (n + 1) * S]))
+    base = chain[0]
+    partners = sorted({(OFFSETS[k][0], OFFSETS[k][1] + m) for m, mine in enumerate(tiles) for k in mine})
+    right = jnp.concatenate([turned_ref[base + i * SLOTS + j] for i, j in partners], axis=1)
+    none = jnp.zeros((S, S), jnp.bfloat16)
+    to_a = 0.0
+    for n in range(2 if fine else 1):
+        w = []
+        for m, mine in enumerate(tiles):
+            at = {(OFFSETS[k][0], OFFSETS[k][1] + m): mine[k][n] for k in mine}
+            w.append(jnp.concatenate([at.get(ij, none) for ij in partners], axis=1))
+        w = jnp.concatenate(w, axis=0)
+        to_a = to_a + lax.dot_general(right, w, (((1,), (1,)), ((), ())), preferred_element_type=jnp.float32)
+    for m, a in enumerate(chain):
+        out.append((a * WIDTH, to_a[:SUMF, m * S : (m + 1) * S]))
     return out
 
 
-def direct_sums(a, bins, ks, refs):
-    p_ref, u_ref, v_ref = refs[4:7]
-    ap, au, av = (down(ref, a) for ref in (p_ref, u_ref, v_ref))
-    rows = None
-    out = []
-    fill = jnp.zeros((8 - 3, S), jnp.float32)
-    for k, (b, dx, dy, w) in zip(ks, geometry(a, bins, refs)):
-        at = pl.ds(b, 1)
-        wx = w * dx
-        wy = w * dy
-        p = ap + p_ref[at, :]
-        vals = (p * wx, p * wy, (au - u_ref[at, :]) * wx + (av - v_ref[at, :]) * wy)
-        rows = vals if rows is None else tuple(r + x for r, x in zip(rows, vals))
-        if k != 0:
-            fx, fy, co = (jnp.sum(x, axis=0, keepdims=True) for x in vals)
-            out.append((b, jnp.concatenate([-fx, -fy, co, fill], axis=0)))
-    rows = [jnp.sum(r.T, axis=0, keepdims=True) for r in rows]
-    out.append((a, jnp.concatenate([*rows, fill], axis=0)))
-    return out
-
-
-def interact(many, ks, direct, refs):
+def fill_rows(*rows):
+    return jnp.concatenate([*rows, jnp.zeros((8 - len(rows), S), jnp.float32)], axis=0)
+
+
+def interact(many, ks, fine, refs):
     acc_ref = refs[-1]
-    sums = [pair_sums(a, ks, direct, refs) for a in many]
+    sums = [column_sums(chain, ks, fine, refs) for chain in many]
     for group in sums:
-        for b, val in group:
-            at = pl.ds(pl.multiple_of(b * SUMF, 8), val.shape[0])
+        for row, val in group:
+            at = pl.ds(pl.multiple_of(row, 8), val.shape[0])
             acc_ref[at, :] = acc_ref[at, :] + val
 
 
-def sweep(ring, direct, many, refs):
+def sweep(ring, fine, many, refs):
     c0, c1 = ring + 1, COLS - 2 - ring
     s0, s1 = ring + 3, SLOTS - 4 - ring
-    step = (c1 - c0 + 1) // many
+    wide, tall = c1 - c0 + 1, s1 - s0 + 1
+    step = wide // many
 
     def column(c, carry):
-        def row(s, carry):
-            interact([(c + step * m) * SLOTS + s for m in range(many)], (0, 1, 2, 3, 4), direct, refs)
+        def row(t, carry):
+            a = c * SLOTS + s0 + CHAIN * t
+            interact([[a + step * m * SLOTS + n for n in range(CHAIN)] for m in range(many)], (0, 1, 2, 3, 4), fine, refs)
             return carry
 
-        return lax.fori_loop(s0 - 1, s1 + 1, row, carry)
+        return lax.fori_loop(0, tall // CHAIN, row, carry)
 
     lax.fori_loop(c0, c0 + step, column, 0)
-    n = s1 - s0 + 3
-    total = n + c1 - c0
-    group = 5 if total % 5 == 0 else 3 if total % 3 == 0 else 1
+
+    def bottom(t, carry):
+        interact([[(c0 + 2 * t + m) * SLOTS + s0 - 1] for m in range(2)], (1, 4), fine, refs)
+        return carry
+
+    lax.fori_loop(0, wide // 2, bottom, 0)
+    n = tall + 2
+    total = n + wide - 1
+    group = 5 if total % 5 == 0 else 7 if total % 7 == 0 else 1
 
     def rim(i, carry):
         ts = [i * group + m for m in range(group)]
         at = [jnp.where(t < n, (c0 - 1) * SLOTS + s0 - 1 + t, (c0 + t - n) * SLOTS + s1 + 1) for t in ts]
-        interact(at, (2, 3, 4), direct, refs)
+        interact([[a] for a in at], (2, 3, 4), fine, refs)
         return carry
 
     lax.fori_loop(0, total // group, rim, 0)
 
 
-def gather_rates(x, y, u, v, rho, occ, direct, acc_ref):
+def gather_rates(x, y, u, v, rho, occ, fine, acc_ref):
     def get(f):
-        return acc_ref[pl.ds(f, NB, stride=SUMF), :]
-
-    if direct:
-        fx, fy, comp = get(0), get(1), get(2)
-    else:
-        gx, gy = on_grid(x, y)
-        s1 = get(0)
-        dx = gx * s1 - (get(1) + (get(2) + get(3)))
-        dy = gy * s1 - (get(4) + (get(5) + get(6)))
-        se = get(11) + (get(12) + get(13))
-        comp = u * dx + v * dy - (gx * (get(7) + get(8)) + gy * (get(9) + get(10)) - se)
-        p = SOUND_SQ * (rho - 1.0) * occ
-        sp = get(14) + get(15)
-        fx = p * dx + (gx * sp - (get(16) + (get(17) + get(18))))
-        fy = p * dy + (gy * sp - (get(19) + (get(20) + get(21))))
+        return acc_ref[pl.ds(f, NB, stride=WIDTH), :]
+
+    gx, gy = on_grid(x, y)
+    s1 = get(0)
+    dx = gx * s1 - (get(1) + (get(2) + get(3)))
+    dy = gy * s1 - (get(4) + (get(5) + get(6)))
+    se = get(11) + (get(12) + get(13))
+    comp = u * dx + v * dy - (gx * (get(7) + get(8)) + gy * (get(9) + get(10)) - se)
+    p = SOUND_SQ * (rho - 1.0) * occ
+    sp = get(14) + get(15)
+    fx = p * dx + (gx * sp - (get(16) + (get(17) + get(18))))
+    fy = p * dy + (gy * sp - (get(19) + (get(20) + get(21))))
+    if fine:
+        fx = fx + get(SUMF)
+        fy = fy + get(SUMF + 1)
+        comp = comp + get(SUMF + 2)
     return FORCE_SCALE * fx, FORCE_SCALE * fy - GRAVITY, -FORCE_SCALE * comp
 
 
@@ -198,8 +231,8 @@
         return x, y, ext_ref[2] * occ, ext_ref[3] * occ, rho, occ
 
     x, y, u, v, rho, occ = load()
-    build(x, y, u, v, rho, occ, False, refs)
-    sweep(0, False, 3, refs)
+    build(x, y, u, v, rho, occ, 0, NB, refs)
+    sweep(0, False, 6, refs)
     x, y, u, v, rho, occ = load()
     ax, ay, ar = gather_rates(x, y, u, v, rho, occ, False, acc_ref)
 
@@ -213,8 +246,8 @@
         )
 
     px, py, pu, pv, pr = predicted()
-    build(px, py, pu, pv, pr, occ, True, refs)
-    sweep(1, True, 2, refs)
+    build(px, py, pu, pv, pr, occ, SLOTS, NB - SLOTS, refs)
+    sweep(1, True, 4, refs)
     ax, ay, ar = gather_rates(px, py, pu, pv, pr, occ, True, acc_ref)
     x, y, u, v, rho, occ = load()
     nu = u + TIME_STEP * ax
@@ -252,7 +285,7 @@
             pltpu.VMEM((NB, S), jnp.float32),
             pltpu.VMEM((NB, S), jnp.float32),
             pltpu.VMEM((NB, S), jnp.float32),
-            pltpu.VMEM((NB * SUMF, S), jnp.float32),
+            pltpu.VMEM((NB * WIDTH, S), jnp.float32),
         ],
         name="sph_step",
     )(ext)

time: 146 us -> 129 us (0.88)
  Pallas kernels: 69.6 us -> 52.5 us
    pallas_call x1, Pallas kernels: 69.6 us -> 52.5 us  [sph_step(): pl.pallas_call(step_kernel, out_shape=(jax.ShapeDtypeStruct((5, NX, NY, S...]
where the time goes in v3:
time: 129 us; the launch traced here: 128 us
  Pallas kernels  52.5 us (41%)
  starting transfers between devices  32.6 us (25%)
  blocking collectives  30.2 us (23%)
  waiting for transfers between devices  8.95 us (7%)
  other arithmetic  3.39 us (3%)
    pallas_call x1, Pallas kernels, sph_step(): pl.pallas_call(step_kernel, out_shape=(jax.ShapeDtypeStruct((5, NX, NY, S...  52.5 us
    ppermute x2, starting transfers between devices, swap(): far = lax.ppermute(jnp.where(even, first, last), axis, pairs(1))  26.7 us
    all_to_all x1, blocking collectives, minimum_everywhere(): lax.all_to_all(got, both, 0, 0, tiled=True, axis_index_groups=lines)  20.4 us
    all_to_all x1, blocking collectives, minimum_everywhere(): got = lax.all_to_all(low, both, 0, 0, tiled=True, axis_index_groups=planes)  9.77 us
    ppermute x2, starting transfers between devices, swap(): near = lax.ppermute(jnp.where(even, last, first), axis, pairs(0))  5.87 us
    ppermute x2, waiting for transfers between devices, swap(): far = lax.ppermute(jnp.where(even, first, last), axis, pairs(1))  5.66 us
    ppermute x2, waiting for transfers between devices, swap(): near = lax.ppermute(jnp.where(even, last, first), axis, pairs(0))  3.29 us
  transfers between devices with their start and end apart: 4, of which 2 were waited for; matrix products, arithmetic and copies ran while one was open for 0% of the time, Pallas kernels for 0%

profile of v3, /device:TPU:1, one launch (start us, length us, event | category | flops | bytes accessed | tf_op | source)
XLA Modules:
  0.0 128.3 jit_solution(13525489717721745663)
XLA Ops:
  0.6 0.0 copy-start
  0.7 0.9 select_bitcast_fusion
  1.5 0.0 copy-done
  1.5 0.9 pad_maximum_fusion
  2.4 18.3 %collective-permute-start = (f32[5,2,16,128]{3,2,1,0:T(8,128)S(1)}, f32[5,2,16,128]{3,2,1,0:T(8,128)S(1)}, u32[]{:S(2)}, u32[]{:S(2)}) collective-permute-start(f32[5,2,16,128]{3,2,1,0:T(8,128)S(1)} %get-tuple-element.11), channel_id=1, source_target_pairs={{4,8},{12,16},{20,24},{28,32},{36,40},{44,48},{52,56},{60,64},{68,... | collective-permute-start | bytes 245768 | tf_op jit(solution)/shard_map/ppermute | solution.py:305
  20.8 1.9 %collective-permute-start.1 = (f32[5,2,16,128]{3,2,1,0:T(8,128)S(1)}, f32[5,2,16,128]{3,2,1,0:T(8,128)S(1)}, u32[]{:S(2)}, u32[]{:S(2)}) collective-permute-start(f32[5,2,16,128]{3,2,1,0:T(8,128)S(1)} %get-tuple-element.12), channel_id=1, source_target_pairs={{0,4},{8,12},{16,20},{24,28},{32,36},{40,44},{48,52},{56,60},{64,6... | collective-permute-start | bytes 245768 | tf_op jit(solution)/shard_map/ppermute | solution.py:304
  22.7 0.0 copy-start.1
  22.7 0.0 collective-permute-done
  22.7 3.3 %collective-permute-done.1 = f32[5,2,16,128]{3,2,1,0:T(8,128)S(1)} collective-permute-done((f32[5,2,16,128]{3,2,1,0:T(8,128)S(1)}, f32[5,2,16,128]{3,2,1,0:T(8,128)S(1)}, u32[]{:S(2)}, u32[]{:S(2)}) %collective-permute-start.1) | collective-permute-done | bytes 81952 | tf_op jit(solution)/shard_map/ppermute | solution.py:304
  26.0 0.0 copy-done.1
  26.1 3.9 %collective-permute-start.3 = (f32[5,8,2,128]{3,2,1,0:T(2,128)S(1)}, f32[5,8,2,128]{3,2,1,0:T(2,128)S(1)}, u32[]{:S(2)}, u32[]{:S(2)}) collective-permute-start(f32[5,8,2,128]{3,2,1,0:T(2,128)S(1)} %bitcast.21), channel_id=1, source_target_pairs={{0,1},{2,3},{1,0},{3,2},{4,5},{6,7},{5,4},{7,6},{8,9},{10,11},{9,8... | collective-permute-start | bytes 122888 | tf_op jit(solution)/shard_map/ppermute | solution.py:304
  30.1 8.4 %collective-permute-start.2 = (f32[5,8,2,128]{3,2,1,0:T(2,128)S(1)}, f32[5,8,2,128]{3,2,1,0:T(2,128)S(1)}, u32[]{:S(2)}, u32[]{:S(2)}) collective-permute-start(f32[5,8,2,128]{3,2,1,0:T(2,128)S(1)} %get-tuple-element.6), channel_id=1, source_target_pairs={{1,2},{2,1},{5,6},{6,5},{9,10},{10,9},{13,14},{14,13},{17,18},{18,... | collective-permute-start | bytes 122888 | tf_op jit(solution)/shard_map/ppermute | solution.py:305
  38.4 0.0 collective-permute-done.3
  38.4 5.7 %collective-permute-done.2 = f32[5,8,2,128]{3,2,1,0:T(2,128)S(1)} collective-permute-done((f32[5,8,2,128]{3,2,1,0:T(2,128)S(1)}, f32[5,8,2,128]{3,2,1,0:T(2,128)S(1)}, u32[]{:S(2)}, u32[]{:S(2)}) %collective-permute-start.2) | collective-permute-done | bytes 40992 | tf_op jit(solution)/shard_map/ppermute | solution.py:305
  44.1 0.9 select_maximum_fusion
  45.0 52.5 %sph_step.1 = (f32[5,4,16,128]{3,2,1,0:T(8,128)}, f32[32,128]{1,0:T(8,128)}) custom-call(f32[5,192,128]{2,1,0:T(8,128)} %bitcast.14), custom_call_target="tpu_custom_call" | custom-call | tf_op jit(solution)/shard_map/sph_step/pallas_call | solution.py:269
  97.5 9.8 %all_to_all.15 = f32[32,1,128]{2,1,0:T(1,128)S(1)} all-to-all(f32[32,1,128]{2,1,0:T(1,128)} %bitcast.23), channel_id=1, replica_groups={{0,1,4,5,8,9,12,13,128,129,132,133,136,137,140,141,256,257,260,261,264,..., dimensions={0} | all-to-all | bytes 32768 | tf_op jit(solution)/shard_map/all_to_all | solution.py:317
  107.3 0.1 reduce_min.18
  107.3 20.4 %all_to_all.16 = f32[16,1,128]{2,1,0:T(1,128)S(1)} all-to-all(f32[16,1,128]{2,1,0:T(1,128)S(1)} %broadcast_in_dim.17), channel_id=1, replica_groups={{0,2,16,18,32,34,48,50,64,66,80,82,96,98,112,114},{1,3,17,19,33,35,49,5..., dimensions={0} | all-to-all | bytes 16384 | tf_op jit(solution)/shard_map/all_to_all | solution.py:319
  127.7 0.6 reduce_min.19
  (6 shorter events, 0.1 us)
Async XLA Ops:
  0.6 0.9 copy-start
  2.4 20.3 %collective-permute-start = (f32[5,2,16,128]{3,2,1,0:T(8,128)S(1)}, f32[5,2,16,128]{3,2,1,0:T(8,128)S(1)}, u32[]{:S(2)}, u32[]{:S(2)}) collective-permute-start(f32[5,2,16,128]{3,2,1,0:T(8,128)S(1)} %get-tuple-element.11), channel_id=1, source_target_pairs={{4,8},{12,16},{20,24},{28,32},{36,40},{44,48},{52,56},{60,64},{68,... | collective-permute-start | bytes 245768 | tf_op jit(solution)/shard_map/ppermute | solution.py:305
  20.8 5.3 %collective-permute-start.1 = (f32[5,2,16,128]{3,2,1,0:T(8,128)S(1)}, f32[5,2,16,128]{3,2,1,0:T(8,128)S(1)}, u32[]{:S(2)}, u32[]{:S(2)}) collective-permute-start(f32[5,2,16,128]{3,2,1,0:T(8,128)S(1)} %get-tuple-element.12), channel_id=1, source_target_pairs={{0,4},{8,12},{16,20},{24,28},{32,36},{40,44},{48,52},{56,60},{64,6... | collective-permute-start | bytes 245768 | tf_op jit(solution)/shard_map/ppermute | solution.py:304
  22.7 3.3 %copy-start.1 = (f32[2,4,16,128]{3,2,1,0:T(8,128)S(1)}, f32[2,4,16,128]{3,2,1,0:T(8,128)}, u32[]{:S(2)}) copy-start(f32[2,4,16,128]{3,2,1,0:T(8,128)} %param.4) | copy-start | bytes 196612
  26.1 12.3 %collective-permute-start.3 = (f32[5,8,2,128]{3,2,1,0:T(2,128)S(1)}, f32[5,8,2,128]{3,2,1,0:T(2,128)S(1)}, u32[]{:S(2)}, u32[]{:S(2)}) collective-permute-start(f32[5,8,2,128]{3,2,1,0:T(2,128)S(1)} %bitcast.21), channel_id=1, source_target_pairs={{0,1},{2,3},{1,0},{3,2},{4,5},{6,7},{5,4},{7,6},{8,9},{10,11},{9,8... | collective-permute-start | bytes 122888 | tf_op jit(solution)/shard_map/ppermute | solution.py:304
  30.1 14.0 %collective-permute-start.2 = (f32[5,8,2,128]{3,2,1,0:T(2,128)S(1)}, f32[5,8,2,128]{3,2,1,0:T(2,128)S(1)}, u32[]{:S(2)}, u32[]{:S(2)}) collective-permute-start(f32[5,8,2,128]{3,2,1,0:T(2,128)S(1)} %get-tuple-element.6), channel_id=1, source_target_pairs={{1,2},{2,1},{5,6},{6,5},{9,10},{10,9},{13,14},{14,13},{17,18},{18,... | collective-permute-start | bytes 122888 | tf_op jit(solution)/shard_map/ppermute | solution.py:305

commit v4 on v3

--- a/solution.py
+++ b/solution.py
@@ -23,8 +23,9 @@
 SLOTS = NY + 2 * HALO + 4
 BASE = HALO + 2
 NB = COLS * SLOTS
+PLANE_ROWS = NB + 8
 SUMF = 24
-WIDTH = SUMF + 8
+EXTRA = 8
 TALL = 32
 OFFSETS = ((0, 0), (0, 1), (1, -1), (1, 0), (1, 1))
 DIRECT = (0, 1)
@@ -54,8 +55,9 @@
 
 
 def build(x, y, u, v, rho, occ, low, high, refs):
-    plane_ref, turned_ref, gx_ref, gy_ref, p_ref, u_ref, v_ref, acc_ref = refs
+    plane_ref, turned_ref, gx_ref, gy_ref, p_ref, u_ref, v_ref, acc_ref, extra_ref = refs
     acc_ref[...] = jnp.zeros_like(acc_ref)
+    extra_ref[...] = jnp.zeros_like(extra_ref)
     gx, gy = on_grid(x, y)
     gx_ref[...] = jnp.where(occ > 0.0, gx, FAR)
     gy_ref[...] = gy
@@ -69,10 +71,10 @@
     rows += split(p, 2) + split(p * gx, 3) + split(p * gy, 3)
     rows += [jnp.zeros((NB, S), jnp.float32)] * (SUMF - len(rows))
     for f, val in enumerate(rows):
-        plane_ref[f * NB : (f + 1) * NB, :] = val
+        plane_ref[f * PLANE_ROWS : f * PLANE_ROWS + NB, :] = val
 
     def turn(r, carry):
-        block = plane_ref[pl.ds(r, SUMF, stride=NB), :]
+        block = plane_ref[pl.ds(r, SUMF, stride=PLANE_ROWS), :]
         block = jnp.concatenate([block, jnp.zeros((TALL - SUMF, S), jnp.float32)], axis=0)
         turned_ref[r] = block.astype(jnp.bfloat16)
         return carry
@@ -99,7 +101,7 @@
 def column_sums(chain, ks, fine, refs):
     turned_ref = refs[1]
     direct = DIRECT if fine else ()
-    p_ref, u_ref, v_ref = refs[4:7]
+    p_ref, u_ref, v_ref, acc_ref, extra_ref = refs[4:9]
     out = []
     tiles = []
     for a in chain:
@@ -122,10 +124,10 @@
             rows = [r + x for r, x in zip(rows, vals)] if rows else list(vals)
             if k != 0:
                 fx, fy, co = (jnp.sum(x, axis=0, keepdims=True) for x in vals)
-                out.append((b * WIDTH + SUMF, fill_rows(-fx, -fy, co)))
+                out.append((extra_ref, b * EXTRA, fill_rows(-fx, -fy, co)))
         if rows:
             rows = [jnp.sum(r.T, axis=0, keepdims=True) for r in rows]
-            out.append((a * WIDTH + SUMF, fill_rows(*rows)))
+            out.append((extra_ref, a * EXTRA, fill_rows(*rows)))
         tiles.append(mine)
         others = [k for k in mine if k != 0]
         to_b = sum(
@@ -134,7 +136,7 @@
         )
         for n, k in enumerate(others):
             b = a + OFFSETS[k][0] * SLOTS + OFFSETS[k][1]
-            out.append((b * WIDTH, to_b[:SUMF, n * S : (n + 1) * S]))
+            out.append((acc_ref, b * SUMF, to_b[:SUMF, n * S : (n + 1) * S]))
     base = chain[0]
     partners = sorted({(OFFSETS[k][0], OFFSETS[k][1] + m) for m, mine in enumerate(tiles) for k in mine})
     right = jnp.concatenate([turned_ref[base + i * SLOTS + j] for i, j in partners], axis=1)
@@ -148,7 +150,7 @@
         w = jnp.concatenate(w, axis=0)
         to_a = to_a + lax.dot_general(right, w, (((1,), (1,)), ((), ())), preferred_element_type=jnp.float32)
     for m, a in enumerate(chain):
-        out.append((a * WIDTH, to_a[:SUMF, m * S : (m + 1) * S]))
+        out.append((acc_ref, a * SUMF, to_a[:SUMF, m * S : (m + 1) * S]))
     return out
 
 
@@ -157,12 +159,11 @@
 
 
 def interact(many, ks, fine, refs):
-    acc_ref = refs[-1]
     sums = [column_sums(chain, ks, fine, refs) for chain in many]
     for group in sums:
-        for row, val in group:
+        for ref, row, val in group:
             at = pl.ds(pl.multiple_of(row, 8), val.shape[0])
-            acc_ref[at, :] = acc_ref[at, :] + val
+            ref[at, :] = ref[at, :] + val
 
 
 def sweep(ring, fine, many, refs):
@@ -199,9 +200,9 @@
     lax.fori_loop(0, total // group, rim, 0)
 
 
-def gather_rates(x, y, u, v, rho, occ, fine, acc_ref):
+def gather_rates(x, y, u, v, rho, occ, fine, acc_ref, extra_ref):
     def get(f):
-        return acc_ref[pl.ds(f, NB, stride=WIDTH), :]
+        return acc_ref[pl.ds(f, NB, stride=SUMF), :]
 
     gx, gy = on_grid(x, y)
     s1 = get(0)
@@ -214,14 +215,25 @@
     fx = p * dx + (gx * sp - (get(16) + (get(17) + get(18))))
     fy = p * dy + (gy * sp - (get(19) + (get(20) + get(21))))
     if fine:
-        fx = fx + get(SUMF)
-        fy = fy + get(SUMF + 1)
-        comp = comp + get(SUMF + 2)
+        own = [extra_ref[pl.ds(f, NB, stride=EXTRA), :] for f in range(3)]
+        fx = fx + own[0]
+        fy = fy + own[1]
+        comp = comp + own[2]
     return FORCE_SCALE * fx, FORCE_SCALE * fy - GRAVITY, -FORCE_SCALE * comp
 
 
-def step_kernel(ext_ref, new_ref, low_ref, *refs):
-    acc_ref = refs[-1]
+def step_kernel(mid_ref, before_ref, after_ref, below_ref, above_ref, new_ref, low_ref, ext_ref, *refs):
+    edge = jnp.zeros((BASE - HALO, S), jnp.float32)
+    for f in range(5):
+        for c in range(COLS):
+            if c < HALO:
+                mid = before_ref[f, c]
+            elif c < HALO + NX:
+                mid = mid_ref[f, c - HALO]
+            else:
+                mid = after_ref[f, c - HALO - NX]
+            rows = [edge, below_ref[f, c], mid, above_ref[f, c], edge]
+            ext_ref[f, c * SLOTS : (c + 1) * SLOTS, :] = jnp.concatenate(rows, axis=0)
 
     def load():
         rho = ext_ref[4]
@@ -234,7 +246,7 @@
     build(x, y, u, v, rho, occ, 0, NB, refs)
     sweep(0, False, 6, refs)
     x, y, u, v, rho, occ = load()
-    ax, ay, ar = gather_rates(x, y, u, v, rho, occ, False, acc_ref)
+    ax, ay, ar = gather_rates(x, y, u, v, rho, occ, False, *refs[-2:])
 
     def predicted():
         return (
@@ -248,7 +260,7 @@
     px, py, pu, pv, pr = predicted()
     build(px, py, pu, pv, pr, occ, SLOTS, NB - SLOTS, refs)
     sweep(1, True, 4, refs)
-    ax, ay, ar = gather_rates(px, py, pu, pv, pr, occ, True, acc_ref)
+    ax, ay, ar = gather_rates(px, py, pu, pv, pr, occ, True, *refs[-2:])
     x, y, u, v, rho, occ = load()
     nu = u + TIME_STEP * ax
     nv = v + TIME_STEP * ay
@@ -265,30 +277,32 @@
     low_ref[...] = jnp.broadcast_to(jnp.min(jnp.concatenate(lows, axis=0)), low_ref.shape)
 
 
-def sph_step(ext):
+def sph_step(*pieces):
     return pl.pallas_call(
         step_kernel,
         out_shape=(
             jax.ShapeDtypeStruct((5, NX, NY, S), jnp.float32),
             jax.ShapeDtypeStruct((PLANE, S), jnp.float32),
         ),
-        in_specs=[pl.BlockSpec(memory_space=pltpu.VMEM)],
+        in_specs=[pl.BlockSpec(memory_space=pltpu.VMEM)] * 5,
         out_specs=(
             pl.BlockSpec(memory_space=pltpu.VMEM),
             pl.BlockSpec(memory_space=pltpu.VMEM),
         ),
         scratch_shapes=[
-            pltpu.VMEM((SUMF * NB, S), jnp.float32),
+            pltpu.VMEM((5, NB, S), jnp.float32),
+            pltpu.VMEM((SUMF * PLANE_ROWS, S), jnp.float32),
             pltpu.VMEM((NB, TALL, S), jnp.bfloat16),
             pltpu.VMEM((NB, S), jnp.float32),
             pltpu.VMEM((NB, S), jnp.float32),
             pltpu.VMEM((NB, S), jnp.float32),
             pltpu.VMEM((NB, S), jnp.float32),
             pltpu.VMEM((NB, S), jnp.float32),
-            pltpu.VMEM((NB * WIDTH, S), jnp.float32),
+            pltpu.VMEM((NB * SUMF, S), jnp.float32),
+            pltpu.VMEM((NB * EXTRA, S), jnp.float32),
         ],
         name="sph_step",
-    )(ext)
+    )(*pieces)
 
 
 def swap(x, dim, axis, wrap):
@@ -326,9 +340,7 @@
     before, after = swap(fields, 1, "chan", True)
     wide = jnp.concatenate([before, fields, after], axis=1)
     below, above = swap(wide, 2, "cross", False)
-    ext = jnp.concatenate([below, wide, above], axis=2)
-    ext = jnp.pad(ext, ((0, 0), (0, 0), (BASE - HALO, SLOTS - NY - HALO - BASE), (0, 0)))
-    new_fields, low = sph_step(ext.reshape(5, NB, S))
+    new_fields, low = sph_step(fields, before, after, below, above)
     return (new_fields, minimum_everywhere(low))
 
 

time: 129 us -> 128 us (level)
  waiting for transfers between devices: 8.95 us -> 2.97 us
  starting transfers between devices: 32.6 us -> 37.5 us
  Pallas kernels: 52.5 us -> 49.4 us
  blocking collectives: 30.2 us -> 32.1 us
    ppermute x2, starting transfers between devices: 26.7 us -> 31.6 us  [swap(): far = lax.ppermute(jnp.where(even, first, last), axis, pairs(1))]
    ppermute x2, waiting for transfers between devices: 5.66 us -> 1.95 us  [swap(): far = lax.ppermute(jnp.where(even, first, last), axis, pairs(1))]
    pallas_call x1, Pallas kernels: 52.5 us -> 49.4 us  [sph_step(): pl.pallas_call(step_kernel, out_shape=(jax.ShapeDtypeStruct((5, NX, NY, S...]
    ppermute x2, waiting for transfers between devices: 3.29 us -> 1.02 us  [swap(): near = lax.ppermute(jnp.where(even, last, first), axis, pairs(0))]
  transfers between devices with their start and end apart: 4 -> 4, of which waited for: 2 -> 3; matrix products, arithmetic and copies ran while one was open for 0% -> 0% of each run, Pallas kernels for 0% -> 0%
where the time goes in v4:
time: 128 us; the launch traced here: 127 us
  Pallas kernels  49.4 us (39%)
  starting transfers between devices  37.5 us (29%)
  blocking collectives  32.1 us (25%)
  other arithmetic  3.1 us (2%)
  waiting for transfers between devices  2.97 us (2%)
    pallas_call x1, Pallas kernels, sph_step(): pl.pallas_call(step_kernel, out_shape=(jax.ShapeDtypeStruct((5, NX, NY, S...  49.4 us
    ppermute x2, starting transfers between devices, swap(): far = lax.ppermute(jnp.where(even, first, last), axis, pairs(1))  31.6 us
    all_to_all x1, blocking collectives, minimum_everywhere(): lax.all_to_all(got, both, 0, 0, tiled=True, axis_index_groups=lines)  21.4 us
    all_to_all x1, blocking collectives, minimum_everywhere(): got = lax.all_to_all(low, both, 0, 0, tiled=True, axis_index_groups=planes)  10.7 us
    ppermute x2, starting transfers between devices, swap(): near = lax.ppermute(jnp.where(even, last, first), axis, pairs(0))  5.93 us
  transfers between devices with their start and end apart: 4, of which 3 were waited for; matrix products, arithmetic and copies ran while one was open for 0% of the time, Pallas kernels for 0%

profile of v4, /device:TPU:1, one launch (start us, length us, event | category | flops | bytes accessed | tf_op | source)
XLA Modules:
  0.0 127.2 jit_solution(3067222203488644435)
XLA Ops:
  0.6 0.0 copy-start.3
  0.7 0.9 select_bitcast_fusion
  1.5 0.0 copy-done.3
  1.5 0.9 pad_maximum_fusion.mid_ref
  2.4 0.0 copy-start
  2.4 0.6 copy-done
  3.0 4.0 %collective-permute-start.1 = (f32[5,2,16,128]{3,2,1,0:T(8,128)S(1)}, f32[5,2,16,128]{3,2,1,0:T(8,128)S(1)}, u32[]{:S(2)}, u32[]{:S(2)}) collective-permute-start(f32[5,2,16,128]{3,2,1,0:T(8,128)S(1)} %get-tuple-element.11), channel_id=1, source_target_pairs={{0,4},{8,12},{16,20},{24,28},{32,36},{40,44},{48,52},{56,60},{64,6... | collective-permute-start | bytes 245768 | tf_op jit(solution)/shard_map/ppermute | solution.py:318
  7.1 16.7 %collective-permute-start = (f32[5,2,16,128]{3,2,1,0:T(8,128)S(1)}, f32[5,2,16,128]{3,2,1,0:T(8,128)S(1)}, u32[]{:S(2)}, u32[]{:S(2)}) collective-permute-start(f32[5,2,16,128]{3,2,1,0:T(8,128)S(1)} %get-tuple-element.12), channel_id=1, source_target_pairs={{4,8},{12,16},{20,24},{28,32},{36,40},{44,48},{52,56},{60,64},{68,... | collective-permute-start | bytes 245768 | tf_op jit(solution)/shard_map/ppermute | solution.py:319
  23.8 0.0 copy-start.4
  23.8 0.0 collective-permute-done.1
  23.8 1.8 %collective-permute-done = f32[5,2,16,128]{3,2,1,0:T(8,128)S(1)} collective-permute-done((f32[5,2,16,128]{3,2,1,0:T(8,128)S(1)}, f32[5,2,16,128]{3,2,1,0:T(8,128)S(1)}, u32[]{:S(2)}, u32[]{:S(2)}) %collective-permute-start) | collective-permute-done | bytes 81952 | tf_op jit(solution)/shard_map/ppermute | solution.py:319
  25.6 0.0 copy-start.1
  25.6 0.0 copy-start.2
  25.6 0.0 copy-done.4
  25.7 0.6 copy-done.1
  26.2 0.0 copy-done.2
  26.3 14.9 %collective-permute-start.2 = (f32[5,8,2,128]{3,2,1,0:T(2,128)S(1)}, f32[5,8,2,128]{3,2,1,0:T(2,128)S(1)}, u32[]{:S(2)}, u32[]{:S(2)}) collective-permute-start(f32[5,8,2,128]{3,2,1,0:T(2,128)S(1)} %bitcast.19), channel_id=1, source_target_pairs={{1,2},{2,1},{5,6},{6,5},{9,10},{10,9},{13,14},{14,13},{17,18},{18,... | collective-permute-start | bytes 122888 | tf_op jit(solution)/shard_map/ppermute | solution.py:319
  41.2 1.9 %collective-permute-start.3 = (f32[5,8,2,128]{3,2,1,0:T(2,128)S(1)}, f32[5,8,2,128]{3,2,1,0:T(2,128)S(1)}, u32[]{:S(2)}, u32[]{:S(2)}) collective-permute-start(f32[5,8,2,128]{3,2,1,0:T(2,128)S(1)} %get-tuple-element.6), channel_id=1, source_target_pairs={{0,1},{2,3},{1,0},{3,2},{4,5},{6,7},{5,4},{7,6},{8,9},{10,11},{9,8... | collective-permute-start | bytes 122888 | tf_op jit(solution)/shard_map/ppermute | solution.py:318
  43.1 0.2 collective-permute-done.2
  43.3 1.0 collective-permute-done.3
  44.3 0.7 broadcast_select_fusion
  45.0 49.4 %sph_step.1 = (f32[5,4,16,128]{3,2,1,0:T(8,128)}, f32[32,128]{1,0:T(8,128)}) custom-call(f32[5,4,16,128]{3,2,1,0:T(8,128)} %copy-done, f32[5,2,16,128]{3,2,1,0:T(8,128)} %copy-done.2, f32[5,2,16,128]{3,2,1,0:T(8,128)} %copy-done.1, f32[5,8,2,128]{3,2,1,0:T(2,128)} %bitcast.14, f32[5,8,2,128]{3,2,1,0:T(2,128)} %bitcast.13), custom_call_target="tpu_custom_call" | custom-call | tf_op jit(solution)/shard_map/sph_step/pallas_call | solution.py:281
  94.4 10.7 %all_to_all.15 = f32[32,1,128]{2,1,0:T(1,128)S(1)} all-to-all(f32[32,1,128]{2,1,0:T(1,128)} %bitcast.21), channel_id=1, replica_groups={{0,1,4,5,8,9,12,13,128,129,132,133,136,137,140,141,256,257,260,261,264,..., dimensions={0} | all-to-all | bytes 32768 | tf_op jit(solution)/shard_map/all_to_all | solution.py:331
  105.1 0.1 reduce_min.18
  105.1 21.4 %all_to_all.16 = f32[16,1,128]{2,1,0:T(1,128)S(1)} all-to-all(f32[16,1,128]{2,1,0:T(1,128)S(1)} %broadcast_in_dim.17), channel_id=1, replica_groups={{0,2,16,18,32,34,48,50,64,66,80,82,96,98,112,114},{1,3,17,19,33,35,49,5..., dimensions={0} | all-to-all | bytes 16384 | tf_op jit(solution)/shard_map/all_to_all | solution.py:333
  126.6 0.6 reduce_min.19
  (5 shorter events, 0.1 us)
Async XLA Ops:
  0.6 0.9 copy-start.3
  2.4 0.7 copy-start
  3.0 20.7 %collective-permute-start.1 = (f32[5,2,16,128]{3,2,1,0:T(8,128)S(1)}, f32[5,2,16,128]{3,2,1,0:T(8,128)S(1)}, u32[]{:S(2)}, u32[]{:S(2)}) collective-permute-start(f32[5,2,16,128]{3,2,1,0:T(8,128)S(1)} %get-tuple-element.11), channel_id=1, source_target_pairs={{0,4},{8,12},{16,20},{24,28},{32,36},{40,44},{48,52},{56,60},{64,6... | collective-permute-start | bytes 245768 | tf_op jit(solution)/shard_map/ppermute | solution.py:318
  7.1 18.5 %collective-permute-start = (f32[5,2,16,128]{3,2,1,0:T(8,128)S(1)}, f32[5,2,16,128]{3,2,1,0:T(8,128)S(1)}, u32[]{:S(2)}, u32[]{:S(2)}) collective-permute-start(f32[5,2,16,128]{3,2,1,0:T(8,128)S(1)} %get-tuple-element.12), channel_id=1, source_target_pairs={{4,8},{12,16},{20,24},{28,32},{36,40},{44,48},{52,56},{60,64},{68,... | collective-permute-start | bytes 245768 | tf_op jit(solution)/shard_map/ppermute | solution.py:319
  23.8 1.8 %copy-start.4 = (f32[2,4,16,128]{3,2,1,0:T(8,128)S(1)}, f32[2,4,16,128]{3,2,1,0:T(8,128)}, u32[]{:S(2)}) copy-start(f32[2,4,16,128]{3,2,1,0:T(8,128)} %param.4) | copy-start | bytes 196612
  25.6 0.6 copy-start.1
  25.6 0.7 copy-start.2
  26.3 17.0 %collective-permute-start.2 = (f32[5,8,2,128]{3,2,1,0:T(2,128)S(1)}, f32[5,8,2,128]{3,2,1,0:T(2,128)S(1)}, u32[]{:S(2)}, u32[]{:S(2)}) collective-permute-start(f32[5,8,2,128]{3,2,1,0:T(2,128)S(1)} %bitcast.19), channel_id=1, source_target_pairs={{1,2},{2,1},{5,6},{6,5},{9,10},{10,9},{13,14},{14,13},{17,18},{18,... | collective-permute-start | bytes 122888 | tf_op jit(solution)/shard_map/ppermute | solution.py:319
  41.2 3.1 %collective-permute-start.3 = (f32[5,8,2,128]{3,2,1,0:T(2,128)S(1)}, f32[5,8,2,128]{3,2,1,0:T(2,128)S(1)}, u32[]{:S(2)}, u32[]{:S(2)}) collective-permute-start(f32[5,8,2,128]{3,2,1,0:T(2,128)S(1)} %get-tuple-element.6), channel_id=1, source_target_pairs={{0,1},{2,3},{1,0},{3,2},{4,5},{6,7},{5,4},{7,6},{8,9},{10,11},{9,8... | collective-permute-start | bytes 122888 | tf_op jit(solution)/shard_map/ppermute | solution.py:318

commit v5 on v4

--- a/solution.py
+++ b/solution.py
@@ -30,6 +30,7 @@
 OFFSETS = ((0, 0), (0, 1), (1, -1), (1, 0), (1, 1))
 DIRECT = (0, 1)
 CHAIN = 2
+OWN = HALO * SLOTS
 FAR = 1000.0
 PLANE = 32
 
@@ -44,8 +45,8 @@
     return out
 
 
-def on_grid(x, y):
-    row = lax.broadcasted_iota(jnp.int32, (NB, S), 0)
+def on_grid(x, y, first=0):
+    row = first + lax.broadcasted_iota(jnp.int32, x.shape, 0)
     col = (row * 171) >> 12
     slot = row - col * SLOTS
     return (
@@ -54,24 +55,26 @@
     )
 
 
-def build(x, y, u, v, rho, occ, low, high, refs):
+def build(x, y, u, v, rho, occ, first, low, high, refs):
     plane_ref, turned_ref, gx_ref, gy_ref, p_ref, u_ref, v_ref, acc_ref, extra_ref = refs
     acc_ref[...] = jnp.zeros_like(acc_ref)
     extra_ref[...] = jnp.zeros_like(extra_ref)
-    gx, gy = on_grid(x, y)
-    gx_ref[...] = jnp.where(occ > 0.0, gx, FAR)
-    gy_ref[...] = gy
+    gx, gy = on_grid(x, y, first)
+    n = x.shape[0]
+    at = slice(first, first + n)
+    gx_ref[at] = jnp.where(occ > 0.0, gx, FAR)
+    gy_ref[at] = gy
     p = SOUND_SQ * (rho - 1.0) * occ
-    p_ref[...] = p
-    u_ref[...] = u
-    v_ref[...] = v
+    p_ref[at] = p
+    u_ref[at] = u
+    v_ref[at] = v
     gx = gx * occ
     gy = gy * occ
     rows = [occ] + split(gx, 3) + split(gy, 3) + split(u, 2) + split(v, 2) + split(u * gx + v * gy, 3)
     rows += split(p, 2) + split(p * gx, 3) + split(p * gy, 3)
-    rows += [jnp.zeros((NB, S), jnp.float32)] * (SUMF - len(rows))
+    rows += [jnp.zeros((n, S), jnp.float32)] * (SUMF - len(rows))
     for f, val in enumerate(rows):
-        plane_ref[f * PLANE_ROWS : f * PLANE_ROWS + NB, :] = val
+        plane_ref[f * PLANE_ROWS + first : f * PLANE_ROWS + first + n, :] = val
 
     def turn(r, carry):
         block = plane_ref[pl.ds(r, SUMF, stride=PLANE_ROWS), :]
@@ -89,8 +92,8 @@
     for b in bins:
         dx = ax - gx_ref[pl.ds(b, 1), :]
         dy = ay - gy_ref[pl.ds(b, 1), :]
-        t = jnp.maximum(dx * dx + dy * dy, 1e-30)
-        q = jnp.maximum(1.0 - t * lax.rsqrt(t), 0.0)
+        t = dx * dx + dy * dy
+        q = jnp.maximum(1.0 - t * lax.rsqrt(jnp.maximum(t, 1e-30)), 0.0)
         yield b, dx, dy, q * q * q
 
 
@@ -166,7 +169,47 @@
             ref[at, :] = ref[at, :] + val
 
 
-def sweep(ring, fine, many, refs):
+def chains(bins):
+    return [[a + n for n in range(CHAIN)] for a in bins]
+
+
+ALL = (0, 1, 2, 3, 4)
+NEXT = (2, 3, 4)
+SAME = (0, 1)
+LOW, TOP = BASE + 1, BASE + NY - CHAIN
+
+
+def sweep_inner(refs):
+    def row(t, carry):
+        s = LOW + CHAIN * t
+        interact(chains([c * SLOTS + s for c in range(HALO, HALO + NX - 1)]), ALL, False, refs)
+        interact(chains([(HALO + NX - 1) * SLOTS + s]), SAME, False, refs)
+        return carry
+
+    lax.fori_loop(0, (NY - 2) // CHAIN, row, 0)
+
+
+def sweep_outer(refs):
+    last = HALO + NX
+
+    def side(t, carry):
+        s = LOW - CHAIN + 3 * CHAIN * t
+        bins = [c * SLOTS + s + CHAIN * m for m in range(3) for c in (HALO - 1, last)]
+        interact(chains(bins), ALL, False, refs)
+        return carry
+
+    lax.fori_loop(0, (NY + 2) // (3 * CHAIN), side, 0)
+
+    def end(t, carry):
+        s = LOW - CHAIN + t * (NY)
+        interact(chains([c * SLOTS + s for c in range(HALO, last)]), ALL, False, refs)
+        return carry
+
+    lax.fori_loop(0, 2, end, 0)
+    interact(chains([(last - 1) * SLOTS + LOW + CHAIN * m for m in range((NY - 2) // CHAIN)]), NEXT, False, refs)
+
+
+def sweep_all(ring, fine, many, refs):
     c0, c1 = ring + 1, COLS - 2 - ring
     s0, s1 = ring + 3, SLOTS - 4 - ring
     wide, tall = c1 - c0 + 1, s1 - s0 + 1
@@ -175,12 +218,18 @@
     def column(c, carry):
         def row(t, carry):
             a = c * SLOTS + s0 + CHAIN * t
-            interact([[a + step * m * SLOTS + n for n in range(CHAIN)] for m in range(many)], (0, 1, 2, 3, 4), fine, refs)
+            interact(chains([a + step * m * SLOTS for m in range(many)]), ALL, fine, refs)
             return carry
 
         return lax.fori_loop(0, tall // CHAIN, row, carry)
 
     lax.fori_loop(c0, c0 + step, column, 0)
+
+
+def sweep_rim(ring, fine, refs):
+    c0, c1 = ring + 1, COLS - 2 - ring
+    s0, s1 = ring + 3, SLOTS - 4 - ring
+    wide, tall = c1 - c0 + 1, s1 - s0 + 1
 
     def bottom(t, carry):
         interact([[(c0 + 2 * t + m) * SLOTS + s0 - 1] for m in range(2)], (1, 4), fine, refs)
@@ -194,7 +243,7 @@
     def rim(i, carry):
         ts = [i * group + m for m in range(group)]
         at = [jnp.where(t < n, (c0 - 1) * SLOTS + s0 - 1 + t, (c0 + t - n) * SLOTS + s1 + 1) for t in ts]
-        interact([[a] for a in at], (2, 3, 4), fine, refs)
+        interact([[a] for a in at], NEXT, fine, refs)
         return carry
 
     lax.fori_loop(0, total // group, rim, 0)
@@ -222,7 +271,8 @@
     return FORCE_SCALE * fx, FORCE_SCALE * fy - GRAVITY, -FORCE_SCALE * comp
 
 
-def step_kernel(mid_ref, before_ref, after_ref, below_ref, above_ref, new_ref, low_ref, ext_ref, *refs):
+def step_kernel(mid_ref, before_ref, after_ref, below_ref, above_ref, inner_ref, new_ref, low_ref, ext_ref, *refs):
+    acc_ref = refs[-2]
     edge = jnp.zeros((BASE - HALO, S), jnp.float32)
     for f in range(5):
         for c in range(COLS):
@@ -243,8 +293,10 @@
         return x, y, ext_ref[2] * occ, ext_ref[3] * occ, rho, occ
 
     x, y, u, v, rho, occ = load()
-    build(x, y, u, v, rho, occ, 0, NB, refs)
-    sweep(0, False, 6, refs)
+    build(x, y, u, v, rho, occ, 0, 0, NB, refs)
+    acc_ref[OWN * SUMF : (OWN + NX * SLOTS) * SUMF, :] = inner_ref[...]
+    sweep_outer(refs)
+    sweep_rim(0, False, refs)
     x, y, u, v, rho, occ = load()
     ax, ay, ar = gather_rates(x, y, u, v, rho, occ, False, *refs[-2:])
 
@@ -258,8 +310,9 @@
         )
 
     px, py, pu, pv, pr = predicted()
-    build(px, py, pu, pv, pr, occ, SLOTS, NB - SLOTS, refs)
-    sweep(1, True, 4, refs)
+    build(px, py, pu, pv, pr, occ, 0, SLOTS, NB - SLOTS, refs)
+    sweep_all(1, True, 4, refs)
+    sweep_rim(1, True, refs)
     ax, ay, ar = gather_rates(px, py, pu, pv, pr, occ, True, *refs[-2:])
     x, y, u, v, rho, occ = load()
     nu = u + TIME_STEP * ax
@@ -277,6 +330,43 @@
     low_ref[...] = jnp.broadcast_to(jnp.min(jnp.concatenate(lows, axis=0)), low_ref.shape)
 
 
+def scratch():
+    return [
+        pltpu.VMEM((SUMF * PLANE_ROWS, S), jnp.float32),
+        pltpu.VMEM((NB, TALL, S), jnp.bfloat16),
+        *[pltpu.VMEM((NB, S), jnp.float32) for _ in range(5)],
+        pltpu.VMEM((NB * SUMF, S), jnp.float32),
+        pltpu.VMEM((NB * EXTRA, S), jnp.float32),
+    ]
+
+
+def inner_kernel(mid_ref, inner_ref, *refs):
+    edge = jnp.zeros((BASE, S), jnp.float32)
+
+    def grid(f):
+        return jnp.concatenate([rows for c in range(NX) for rows in (edge, mid_ref[f, c], edge)], axis=0)
+
+    rho = grid(4)
+    occ = jnp.where(rho > 0.0, 1.0, 0.0)
+    x = (grid(0) - 0.5) * occ
+    y = (grid(1) - 0.5) * occ
+    build(x, y, grid(2) * occ, grid(3) * occ, rho, occ, OWN, OWN, OWN + NX * SLOTS, refs)
+    sweep_inner(refs)
+    inner_ref[...] = refs[-2][OWN * SUMF : (OWN + NX * SLOTS) * SUMF, :]
+
+
+def sph_inner(mid):
+    return pl.pallas_call(
+        inner_kernel,
+        out_shape=jax.ShapeDtypeStruct((NX * SLOTS * SUMF, S), jnp.float32),
+        in_specs=[pl.BlockSpec(memory_space=pltpu.VMEM)],
+        out_specs=pl.BlockSpec(memory_space=pltpu.VMEM),
+        scratch_shapes=scratch(),
+        cost_estimate=pl.CostEstimate(flops=8000000000, transcendentals=0, bytes_accessed=1000000),
+        name="sph_inner",
+    )(mid)
+
+
 def sph_step(*pieces):
     return pl.pallas_call(
         step_kernel,
@@ -284,23 +374,12 @@
             jax.ShapeDtypeStruct((5, NX, NY, S), jnp.float32),
             jax.ShapeDtypeStruct((PLANE, S), jnp.float32),
         ),
-        in_specs=[pl.BlockSpec(memory_space=pltpu.VMEM)] * 5,
+        in_specs=[pl.BlockSpec(memory_space=pltpu.VMEM)] * 6,
         out_specs=(
             pl.BlockSpec(memory_space=pltpu.VMEM),
             pl.BlockSpec(memory_space=pltpu.VMEM),
         ),
-        scratch_shapes=[
-            pltpu.VMEM((5, NB, S), jnp.float32),
-            pltpu.VMEM((SUMF * PLANE_ROWS, S), jnp.float32),
-            pltpu.VMEM((NB, TALL, S), jnp.bfloat16),
-            pltpu.VMEM((NB, S), jnp.float32),
-            pltpu.VMEM((NB, S), jnp.float32),
-            pltpu.VMEM((NB, S), jnp.float32),
-            pltpu.VMEM((NB, S), jnp.float32),
-            pltpu.VMEM((NB, S), jnp.float32),
-            pltpu.VMEM((NB * SUMF, S), jnp.float32),
-            pltpu.VMEM((NB * EXTRA, S), jnp.float32),
-        ],
+        scratch_shapes=[pltpu.VMEM((5, NB, S), jnp.float32), *scratch()],
         name="sph_step",
     )(*pieces)
 
@@ -340,7 +419,7 @@
     before, after = swap(fields, 1, "chan", True)
     wide = jnp.concatenate([before, fields, after], axis=1)
     below, above = swap(wide, 2, "cross", False)
-    new_fields, low = sph_step(fields, before, after, below, above)
+    new_fields, low = sph_step(fields, before, after, below, above, sph_inner(fields))
     return (new_fields, minimum_everywhere(low))
 
 

time: 128 us -> 126 us (0.984)
  blocking collectives: 32.1 us -> 29.3 us
  Pallas kernels: 49.4 us -> 51.7 us
    pallas_call x0 -> x1, Pallas kernels: none -> 11.3 us  [sph_inner(): pl.pallas_call(inner_kernel, out_shape=jax.ShapeDtypeStruct((NX * SLOTS *...]
    pallas_call x1, Pallas kernels: 49.4 us -> 40.4 us  [sph_step(): pl.pallas_call(step_kernel, out_shape=(jax.ShapeDtypeStruct((5, NX, NY, S...]
    all_to_all x1, blocking collectives: 21.4 us -> 18.2 us  [minimum_everywhere(): lax.all_to_all(got, both, 0, 0, tiled=True, axis_index_groups=lines)]
  transfers between devices with their start and end apart: 4 -> 4, of which waited for: 3 -> 1; matrix products, arithmetic and copies ran while one was open for 0% -> 0% of each run, Pallas kernels for 0% -> 9%
where the time goes in v5:
time: 126 us; the launch traced here: 125 us
  Pallas kernels  51.7 us (41%)
  starting transfers between devices  37.6 us (30%)
  blocking collectives  29.3 us (23%)
  other arithmetic  3.96 us (3%)
  waiting for transfers between devices  1.8 us (1%)
    pallas_call x1, Pallas kernels, sph_step(): pl.pallas_call(step_kernel, out_shape=(jax.ShapeDtypeStruct((5, NX, NY, S...  40.4 us
    ppermute x2, starting transfers between devices, swap(): far = lax.ppermute(jnp.where(even, first, last), axis, pairs(1))  31.6 us
    all_to_all x1, blocking collectives, minimum_everywhere(): lax.all_to_all(got, both, 0, 0, tiled=True, axis_index_groups=lines)  18.2 us
    pallas_call x1, Pallas kernels, sph_inner(): pl.pallas_call(inner_kernel, out_shape=jax.ShapeDtypeStruct((NX * SLOTS *...  11.3 us
    all_to_all x1, blocking collectives, minimum_everywhere(): got = lax.all_to_all(low, both, 0, 0, tiled=True, axis_index_groups=planes)  11.1 us
    ppermute x2, starting transfers between devices, swap(): near = lax.ppermute(jnp.where(even, last, first), axis, pairs(0))  5.94 us
  transfers between devices with their start and end apart: 4, of which 1 were waited for; matrix products, arithmetic and copies ran while one was open for 0% of the time, Pallas kernels for 9%

profile of v5, /device:TPU:1, one launch (start us, length us, event | category | flops | bytes accessed | tf_op | source)
XLA Modules:
  0.0 125.1 jit_solution(5219207624797264631)
XLA Ops:
  0.6 0.8 select_bitcast_fusion
  1.5 0.9 pad_maximum_fusion.mid_ref
  2.4 0.0 copy-start
  2.4 4.0 %collective-permute-start.1 = (f32[5,2,16,128]{3,2,1,0:T(8,128)S(1)}, f32[5,2,16,128]{3,2,1,0:T(8,128)S(1)}, u32[]{:S(2)}, u32[]{:S(2)}) collective-permute-start(f32[5,2,16,128]{3,2,1,0:T(8,128)S(1)} %get-tuple-element.11), channel_id=1, source_target_pairs={{0,4},{8,12},{16,20},{24,28},{32,36},{40,44},{48,52},{56,60},{64,6... | collective-permute-start | bytes 245768 | tf_op jit(solution)/shard_map/ppermute | solution.py:397
  6.4 16.7 %collective-permute-start = (f32[5,2,16,128]{3,2,1,0:T(8,128)S(1)}, f32[5,2,16,128]{3,2,1,0:T(8,128)S(1)}, u32[]{:S(2)}, u32[]{:S(2)}) collective-permute-start(f32[5,2,16,128]{3,2,1,0:T(8,128)S(1)} %get-tuple-element.12), channel_id=1, source_target_pairs={{4,8},{12,16},{20,24},{28,32},{36,40},{44,48},{52,56},{60,64},{68,... | collective-permute-start | bytes 245768 | tf_op jit(solution)/shard_map/ppermute | solution.py:398
  23.1 0.0 collective-permute-done.1
  23.2 1.8 %collective-permute-done = f32[5,2,16,128]{3,2,1,0:T(8,128)S(1)} collective-permute-done((f32[5,2,16,128]{3,2,1,0:T(8,128)S(1)}, f32[5,2,16,128]{3,2,1,0:T(8,128)S(1)}, u32[]{:S(2)}, u32[]{:S(2)}) %collective-permute-start) | collective-permute-done | bytes 81952 | tf_op jit(solution)/shard_map/ppermute | solution.py:398
  25.0 0.0 copy-start.1
  25.0 0.0 copy-start.2
  25.0 0.9 broadcast_select_fusion.2
  25.9 14.9 %collective-permute-start.2 = (f32[5,8,2,128]{3,2,1,0:T(2,128)S(1)}, f32[5,8,2,128]{3,2,1,0:T(2,128)S(1)}, u32[]{:S(2)}, u32[]{:S(2)}) collective-permute-start(f32[5,8,2,128]{3,2,1,0:T(2,128)S(1)} %bitcast.19), channel_id=1, source_target_pairs={{1,2},{2,1},{5,6},{6,5},{9,10},{10,9},{13,14},{14,13},{17,18},{18,... | collective-permute-start | bytes 122888 | tf_op jit(solution)/shard_map/ppermute | solution.py:398
  40.8 1.9 %collective-permute-start.3 = (f32[5,8,2,128]{3,2,1,0:T(2,128)S(1)}, f32[5,8,2,128]{3,2,1,0:T(2,128)S(1)}, u32[]{:S(2)}, u32[]{:S(2)}) collective-permute-start(f32[5,8,2,128]{3,2,1,0:T(2,128)S(1)} %get-tuple-element.6), channel_id=1, source_target_pairs={{0,1},{2,3},{1,0},{3,2},{4,5},{6,7},{5,4},{7,6},{8,9},{10,11},{9,8... | collective-permute-start | bytes 122888 | tf_op jit(solution)/shard_map/ppermute | solution.py:397
  42.8 0.0 copy-done
  42.8 11.3 %sph_inner.1.inner_ref = f32[2304,128]{1,0:T(8,128)} custom-call(f32[5,4,16,128]{3,2,1,0:T(8,128)} %copy-done), custom_call_target="tpu_custom_call" | custom-call | flops 8000000000 | bytes 1000000 | tf_op jit(solution)/shard_map/sph_inner/pallas_call | solution.py:359
  54.1 0.0 copy-done.1
  54.1 0.0 copy-done.2
  54.1 0.0 collective-permute-done.2
  54.1 0.0 collective-permute-done.3
  54.1 0.6 broadcast_select_fusion
  54.8 40.4 %sph_step.1 = (f32[5,4,16,128]{3,2,1,0:T(8,128)}, f32[32,128]{1,0:T(8,128)}) custom-call(f32[5,4,16,128]{3,2,1,0:T(8,128)} %copy-done, f32[5,2,16,128]{3,2,1,0:T(8,128)} %copy-done.2, f32[5,2,16,128]{3,2,1,0:T(8,128)} %copy-done.1, f32[5,8,2,128]{3,2,1,0:T(2,128)} %bitcast.14, f32[5,8,2,128]{3,2,1,0:T(2,128)} %bitcast.13, f32[2304,128]{1,0:T(8,128)} %sph_inner.1.inner_ref), custom_call_target="tpu_custom_call" | custom-call | tf_op jit(solution)/shard_map/sph_step/pallas_call | solution.py:371
  95.2 11.1 %all_to_all.15 = f32[32,1,128]{2,1,0:T(1,128)S(1)} all-to-all(f32[32,1,128]{2,1,0:T(1,128)} %bitcast.21), channel_id=1, replica_groups={{0,1,4,5,8,9,12,13,128,129,132,133,136,137,140,141,256,257,260,261,264,..., dimensions={0} | all-to-all | bytes 32768 | tf_op jit(solution)/shard_map/all_to_all | solution.py:410
  106.2 0.1 reduce_min.18
  106.3 18.2 %all_to_all.16 = f32[16,1,128]{2,1,0:T(1,128)S(1)} all-to-all(f32[16,1,128]{2,1,0:T(1,128)S(1)} %broadcast_in_dim.17), channel_id=1, replica_groups={{0,2,16,18,32,34,48,50,64,66,80,82,96,98,112,114},{1,3,17,19,33,35,49,5..., dimensions={0} | all-to-all | bytes 16384 | tf_op jit(solution)/shard_map/all_to_all | solution.py:412
  124.5 0.6 reduce_min.19
  (4 shorter events, 0.0 us)
Async XLA Ops:
  2.4 40.4 %copy-start = (f32[5,4,16,128]{3,2,1,0:T(8,128)}, f32[5,4,16,128]{3,2,1,0:T(8,128)S(1)}, u32[]{:S(2)}) copy-start(f32[5,4,16,128]{3,2,1,0:T(8,128)S(1)} %pad_maximum_fusion.mid_ref) | copy-start | bytes 491524
  2.4 20.7 %collective-permute-start.1 = (f32[5,2,16,128]{3,2,1,0:T(8,128)S(1)}, f32[5,2,16,128]{3,2,1,0:T(8,128)S(1)}, u32[]{:S(2)}, u32[]{:S(2)}) collective-permute-start(f32[5,2,16,128]{3,2,1,0:T(8,128)S(1)} %get-tuple-element.11), channel_id=1, source_target_pairs={{0,4},{8,12},{16,20},{24,28},{32,36},{40,44},{48,52},{56,60},{64,6... | collective-permute-start | bytes 245768 | tf_op jit(solution)/shard_map/ppermute | solution.py:397
  6.4 18.5 %collective-permute-start = (f32[5,2,16,128]{3,2,1,0:T(8,128)S(1)}, f32[5,2,16,128]{3,2,1,0:T(8,128)S(1)}, u32[]{:S(2)}, u32[]{:S(2)}) collective-permute-start(f32[5,2,16,128]{3,2,1,0:T(8,128)S(1)} %get-tuple-element.12), channel_id=1, source_target_pairs={{4,8},{12,16},{20,24},{28,32},{36,40},{44,48},{52,56},{60,64},{68,... | collective-permute-start | bytes 245768 | tf_op jit(solution)/shard_map/ppermute | solution.py:398
  25.0 29.1 %copy-start.1 = (f32[5,2,16,128]{3,2,1,0:T(8,128)}, f32[5,2,16,128]{3,2,1,0:T(8,128)S(1)}, u32[]{:S(2)}) copy-start(f32[5,2,16,128]{3,2,1,0:T(8,128)S(1)} %get-tuple-element.9.after_ref) | copy-start | bytes 245764
  25.0 29.1 %copy-start.2 = (f32[5,2,16,128]{3,2,1,0:T(8,128)}, f32[5,2,16,128]{3,2,1,0:T(8,128)S(1)}, u32[]{:S(2)}) copy-start(f32[5,2,16,128]{3,2,1,0:T(8,128)S(1)} %get-tuple-element.10.before_ref) | copy-start | bytes 245764
  25.9 28.2 %collective-permute-start.2 = (f32[5,8,2,128]{3,2,1,0:T(2,128)S(1)}, f32[5,8,2,128]{3,2,1,0:T(2,128)S(1)}, u32[]{:S(2)}, u32[]{:S(2)}) collective-permute-start(f32[5,8,2,128]{3,2,1,0:T(2,128)S(1)} %bitcast.19), channel_id=1, source_target_pairs={{1,2},{2,1},{5,6},{6,5},{9,10},{10,9},{13,14},{14,13},{17,18},{18,... | collective-permute-start | bytes 122888 | tf_op jit(solution)/shard_map/ppermute | solution.py:398
  40.8 13.3 %collective-permute-start.3 = (f32[5,8,2,128]{3,2,1,0:T(2,128)S(1)}, f32[5,8,2,128]{3,2,1,0:T(2,128)S(1)}, u32[]{:S(2)}, u32[]{:S(2)}) collective-permute-start(f32[5,8,2,128]{3,2,1,0:T(2,128)S(1)} %get-tuple-element.6), channel_id=1, source_target_pairs={{0,1},{2,3},{1,0},{3,2},{4,5},{6,7},{5,4},{7,6},{8,9},{10,11},{9,8... | collective-permute-start | bytes 122888 | tf_op jit(solution)/shard_map/ppermute | solution.py:397

commit v6 on v5

--- a/solution.py
+++ b/solution.py
@@ -176,7 +176,7 @@
 ALL = (0, 1, 2, 3, 4)
 NEXT = (2, 3, 4)
 SAME = (0, 1)
-LOW, TOP = BASE + 1, BASE + NY - CHAIN
+LOW = BASE + 1
 
 
 def sweep_inner(refs):
@@ -340,7 +340,8 @@
     ]
 
 
-def inner_kernel(mid_ref, inner_ref, *refs):
+def inner_kernel(mid_ref, inner_ref, tick_ref, *refs):
+    tick_ref[...] = jnp.zeros_like(tick_ref)
     edge = jnp.zeros((BASE, S), jnp.float32)
 
     def grid(f):
@@ -358,9 +359,12 @@
 def sph_inner(mid):
     return pl.pallas_call(
         inner_kernel,
-        out_shape=jax.ShapeDtypeStruct((NX * SLOTS * SUMF, S), jnp.float32),
+        out_shape=(
+            jax.ShapeDtypeStruct((NX * SLOTS * SUMF, S), jnp.float32),
+            jax.ShapeDtypeStruct((8, S), jnp.float32),
+        ),
         in_specs=[pl.BlockSpec(memory_space=pltpu.VMEM)],
-        out_specs=pl.BlockSpec(memory_space=pltpu.VMEM),
+        out_specs=(pl.BlockSpec(memory_space=pltpu.VMEM), pl.BlockSpec(memory_space=pltpu.VMEM)),
         scratch_shapes=scratch(),
         cost_estimate=pl.CostEstimate(flops=8000000000, transcendentals=0, bytes_accessed=1000000),
         name="sph_inner",
@@ -384,18 +388,20 @@
     )(*pieces)
 
 
-def swap(x, dim, axis, wrap):
+def swap(x, dim, axis, wrap, tick=None):
     size, length = lax.axis_size(axis), x.shape[dim]
     even = lax.axis_index(axis) % 2 == 0
     last = lax.slice_in_dim(x, length - HALO, length, axis=dim)
     first = lax.slice_in_dim(x, 0, HALO, axis=dim)
+    if tick is not None:
+        last, first = last + tick, first + tick
 
     def pairs(start):
         ends = [(i, (i + 1) % size) for i in range(start, size if wrap else size - 1, 2)]
         return ends + [(j, i) for i, j in ends]
 
+    far = lax.ppermute(jnp.where(even, first, last), axis, pairs(1))
     near = lax.ppermute(jnp.where(even, last, first), axis, pairs(0))
-    far = lax.ppermute(jnp.where(even, first, last), axis, pairs(1))
     return jnp.where(even, far, near), jnp.where(even, near, far)
 
 
@@ -418,8 +424,9 @@
     fields = jnp.concatenate([positions, velocity, rho[None]], axis=0)
     before, after = swap(fields, 1, "chan", True)
     wide = jnp.concatenate([before, fields, after], axis=1)
-    below, above = swap(wide, 2, "cross", False)
-    new_fields, low = sph_step(fields, before, after, below, above, sph_inner(fields))
+    inner, tick = sph_inner(fields)
+    below, above = swap(wide, 2, "cross", False, tick[0, 0])
+    new_fields, low = sph_step(fields, before, after, below, above, inner)
     return (new_fields, minimum_everywhere(low))
 
 

time: 126 us -> 123 us (0.976)
  starting transfers between devices: 37.6 us -> 31.8 us
  waiting for transfers between devices: 1.8 us -> 3.07 us
    ppermute x2, starting transfers between devices: 31.6 us -> 25.9 us  [swap(): far = lax.ppermute(jnp.where(even, first, last), axis, pairs(1))]
    all_to_all x1, blocking collectives: 18.2 us -> 20.8 us  [minimum_everywhere(): lax.all_to_all(got, both, 0, 0, tiled=True, axis_index_groups=lines)]
    all_to_all x1, blocking collectives: 11.1 us -> 9.43 us  [minimum_everywhere(): got = lax.all_to_all(low, both, 0, 0, tiled=True, axis_index_groups=planes)]
    ppermute x2, waiting for transfers between devices: 1.79 us -> 3.07 us  [swap(): far = lax.ppermute(jnp.where(even, first, last), axis, pairs(1))]
  transfers between devices with their start and end apart: 4 -> 4, of which waited for: 1 -> 1; matrix products, arithmetic and copies ran while one was open for 0% -> 1% of each run, Pallas kernels for 9% -> 9%
where the time goes in v6:
time: 123 us
  Pallas kernels  51.7 us (42%)
  starting transfers between devices  31.8 us (26%)
  blocking collectives  30.2 us (25%)
  other arithmetic  3.75 us (3%)
  waiting for transfers between devices  3.07 us (2%)
  local copies, waits for them, and re-layouts  1.23 us (1%)
    pallas_call x1, Pallas kernels, sph_step(): pl.pallas_call(step_kernel, out_shape=(jax.ShapeDtypeStruct((5, NX, NY, S...  40.4 us
    ppermute x2, starting transfers between devices, swap(): far = lax.ppermute(jnp.where(even, first, last), axis, pairs(1))  25.9 us
    all_to_all x1, blocking collectives, minimum_everywhere(): lax.all_to_all(got, both, 0, 0, tiled=True, axis_index_groups=lines)  20.8 us
    pallas_call x1, Pallas kernels, sph_inner(): pl.pallas_call(inner_kernel, out_shape=(jax.ShapeDtypeStruct((NX * SLOTS...  11.3 us
    all_to_all x1, blocking collectives, minimum_everywhere(): got = lax.all_to_all(low, both, 0, 0, tiled=True, axis_index_groups=planes)  9.43 us
    ppermute x2, starting transfers between devices, swap(): near = lax.ppermute(jnp.where(even, last, first), axis, pairs(0))  5.94 us
    ppermute x2, waiting for transfers between devices, swap(): far = lax.ppermute(jnp.where(even, first, last), axis, pairs(1))  3.07 us
  transfers between devices with their start and end apart: 4, of which 1 were waited for; matrix products, arithmetic and copies ran while one was open for 1% of the time, Pallas kernels for 9%

profile of v6, /device:TPU:1, one launch (start us, length us, event | category | flops | bytes accessed | tf_op | source)
XLA Modules:
  0.0 122.6 jit_solution(15230669482632754471)
XLA Ops:
  0.6 0.8 select_bitcast_fusion
  1.5 0.9 pad_maximum_fusion.mid_ref
  2.4 0.0 copy-start
  2.4 4.0 %collective-permute-start.1 = (f32[5,2,16,128]{3,2,1,0:T(8,128)S(1)}, f32[5,2,16,128]{3,2,1,0:T(8,128)S(1)}, u32[]{:S(2)}, u32[]{:S(2)}) collective-permute-start(f32[5,2,16,128]{3,2,1,0:T(8,128)S(1)} %get-tuple-element.15), channel_id=1, source_target_pairs={{0,4},{8,12},{16,20},{24,28},{32,36},{40,44},{48,52},{56,60},{64,6... | collective-permute-start | bytes 245768 | tf_op jit(solution)/shard_map/ppermute | solution.py:404
  6.4 0.0 copy-start.3
  6.4 0.0 copy-start.4
  6.5 16.8 %collective-permute-start = (f32[5,2,16,128]{3,2,1,0:T(8,128)S(1)}, f32[5,2,16,128]{3,2,1,0:T(8,128)S(1)}, u32[]{:S(2)}, u32[]{:S(2)}) collective-permute-start(f32[5,2,16,128]{3,2,1,0:T(8,128)S(1)} %get-tuple-element.16), channel_id=1, source_target_pairs={{4,8},{12,16},{20,24},{28,32},{36,40},{44,48},{52,56},{60,64},{68,... | collective-permute-start | bytes 245768 | tf_op jit(solution)/shard_map/ppermute | solution.py:403
  23.3 0.0 copy-done
  23.3 11.3 %sph_inner.1 = (f32[2304,128]{1,0:T(8,128)}, f32[8,128]{1,0:T(8,128)}) custom-call(f32[5,4,16,128]{3,2,1,0:T(8,128)} %copy-done), custom_call_target="tpu_custom_call" | custom-call | flops 8000000000 | bytes 1000000 | tf_op jit(solution)/shard_map/sph_inner/pallas_call | solution.py:360
  34.6 1.2 slice.18
  35.8 0.0 collective-permute-done.1
  35.8 0.0 collective-permute-done
  35.8 0.0 copy-start.1
  35.8 0.0 copy-start.2
  35.9 0.0 copy-done.3
  35.9 0.0 copy-done.4
  35.9 0.7 broadcast_select_fusion.2
  36.6 9.1 %collective-permute-start.2 = (f32[5,8,2,128]{3,2,1,0:T(2,128)S(1)}, f32[5,8,2,128]{3,2,1,0:T(2,128)S(1)}, u32[]{:S(2)}, u32[]{:S(2)}) collective-permute-start(f32[5,8,2,128]{3,2,1,0:T(2,128)S(1)} %bitcast.20), channel_id=1, source_target_pairs={{1,2},{2,1},{5,6},{6,5},{9,10},{10,9},{13,14},{14,13},{17,18},{18,... | collective-permute-start | bytes 122888 | tf_op jit(solution)/shard_map/ppermute | solution.py:403
  45.7 1.9 %collective-permute-start.3 = (f32[5,8,2,128]{3,2,1,0:T(2,128)S(1)}, f32[5,8,2,128]{3,2,1,0:T(2,128)S(1)}, u32[]{:S(2)}, u32[]{:S(2)}) collective-permute-start(f32[5,8,2,128]{3,2,1,0:T(2,128)S(1)} %get-tuple-element.10), channel_id=1, source_target_pairs={{0,1},{2,3},{1,0},{3,2},{4,5},{6,7},{5,4},{7,6},{8,9},{10,11},{9,8... | collective-permute-start | bytes 122888 | tf_op jit(solution)/shard_map/ppermute | solution.py:404
  47.6 3.1 %collective-permute-done.2 = f32[5,8,2,128]{3,2,1,0:T(2,128)S(1)} collective-permute-done((f32[5,8,2,128]{3,2,1,0:T(2,128)S(1)}, f32[5,8,2,128]{3,2,1,0:T(2,128)S(1)}, u32[]{:S(2)}, u32[]{:S(2)}) %collective-permute-start.2) | collective-permute-done | bytes 40992 | tf_op jit(solution)/shard_map/ppermute | solution.py:403
  50.7 0.0 collective-permute-done.3
  50.7 0.6 broadcast_select_fusion
  51.3 0.0 copy-done.1
  51.3 0.0 copy-done.2
  51.3 40.4 %sph_step.1 = (f32[5,4,16,128]{3,2,1,0:T(8,128)}, f32[32,128]{1,0:T(8,128)}) custom-call(f32[5,4,16,128]{3,2,1,0:T(8,128)} %copy-done, f32[5,2,16,128]{3,2,1,0:T(8,128)} %copy-done.2, f32[5,2,16,128]{3,2,1,0:T(8,128)} %copy-done.1, f32[5,8,2,128]{3,2,1,0:T(2,128)} %bitcast.15, f32[5,8,2,128]{3,2,1,0:T(2,128)} %bitcast.14, f32[2304,128]{1,0:T(8,128)} %get-tuple-element.7.inner_ref), custom_call_target="tpu_custom_call" | custom-call | tf_op jit(solution)/shard_map/sph_step/pallas_call | solution.py:375
  91.7 9.4 %all_to_all.15 = f32[32,1,128]{2,1,0:T(1,128)S(1)} all-to-all(f32[32,1,128]{2,1,0:T(1,128)} %bitcast.22), channel_id=1, replica_groups={{0,1,4,5,8,9,12,13,128,129,132,133,136,137,140,141,256,257,260,261,264,..., dimensions={0} | all-to-all | bytes 32768 | tf_op jit(solution)/shard_map/all_to_all | solution.py:416
  101.1 0.1 reduce_min.18
  101.2 20.8 %all_to_all.16 = f32[16,1,128]{2,1,0:T(1,128)S(1)} all-to-all(f32[16,1,128]{2,1,0:T(1,128)S(1)} %broadcast_in_dim.17), channel_id=1, replica_groups={{0,2,16,18,32,34,48,50,64,66,80,82,96,98,112,114},{1,3,17,19,33,35,49,5..., dimensions={0} | all-to-all | bytes 16384 | tf_op jit(solution)/shard_map/all_to_all | solution.py:418
  122.0 0.6 reduce_min.19
  (4 shorter events, 0.0 us)
Async XLA Ops:
  2.4 20.9 %copy-start = (f32[5,4,16,128]{3,2,1,0:T(8,128)}, f32[5,4,16,128]{3,2,1,0:T(8,128)S(1)}, u32[]{:S(2)}) copy-start(f32[5,4,16,128]{3,2,1,0:T(8,128)S(1)} %pad_maximum_fusion.mid_ref) | copy-start | bytes 491524
  2.4 33.4 %collective-permute-start.1 = (f32[5,2,16,128]{3,2,1,0:T(8,128)S(1)}, f32[5,2,16,128]{3,2,1,0:T(8,128)S(1)}, u32[]{:S(2)}, u32[]{:S(2)}) collective-permute-start(f32[5,2,16,128]{3,2,1,0:T(8,128)S(1)} %get-tuple-element.15), channel_id=1, source_target_pairs={{0,4},{8,12},{16,20},{24,28},{32,36},{40,44},{48,52},{56,60},{64,6... | collective-permute-start | bytes 245768 | tf_op jit(solution)/shard_map/ppermute | solution.py:404
  6.4 29.4 %copy-start.3 = (f32[2,4,16,128]{3,2,1,0:T(8,128)S(1)}, f32[2,4,16,128]{3,2,1,0:T(8,128)}, u32[]{:S(2)}) copy-start(f32[2,4,16,128]{3,2,1,0:T(8,128)} %param.5) | copy-start | bytes 196612
  6.4 29.4 %copy-start.4 = (f32[2,4,16,128]{3,2,1,0:T(8,128)S(1)}, f32[2,4,16,128]{3,2,1,0:T(8,128)}, u32[]{:S(2)}) copy-start(f32[2,4,16,128]{3,2,1,0:T(8,128)} %param.4) | copy-start | bytes 196612
  6.5 29.4 %collective-permute-start = (f32[5,2,16,128]{3,2,1,0:T(8,128)S(1)}, f32[5,2,16,128]{3,2,1,0:T(8,128)S(1)}, u32[]{:S(2)}, u32[]{:S(2)}) collective-permute-start(f32[5,2,16,128]{3,2,1,0:T(8,128)S(1)} %get-tuple-element.16), channel_id=1, source_target_pairs={{4,8},{12,16},{20,24},{28,32},{36,40},{44,48},{52,56},{60,64},{68,... | collective-permute-start | bytes 245768 | tf_op jit(solution)/shard_map/ppermute | solution.py:403
  35.8 15.5 %copy-start.1 = (f32[5,2,16,128]{3,2,1,0:T(8,128)}, f32[5,2,16,128]{3,2,1,0:T(8,128)S(1)}, u32[]{:S(2)}) copy-start(f32[5,2,16,128]{3,2,1,0:T(8,128)S(1)} %get-tuple-element.13.after_ref) | copy-start | bytes 245764
  35.8 15.5 %copy-start.2 = (f32[5,2,16,128]{3,2,1,0:T(8,128)}, f32[5,2,16,128]{3,2,1,0:T(8,128)S(1)}, u32[]{:S(2)}) copy-start(f32[5,2,16,128]{3,2,1,0:T(8,128)S(1)} %get-tuple-element.14.before_ref) | copy-start | bytes 245764
  36.6 14.1 %collective-permute-start.2 = (f32[5,8,2,128]{3,2,1,0:T(2,128)S(1)}, f32[5,8,2,128]{3,2,1,0:T(2,128)S(1)}, u32[]{:S(2)}, u32[]{:S(2)}) collective-permute-start(f32[5,8,2,128]{3,2,1,0:T(2,128)S(1)} %bitcast.20), channel_id=1, source_target_pairs={{1,2},{2,1},{5,6},{6,5},{9,10},{10,9},{13,14},{14,13},{17,18},{18,... | collective-permute-start | bytes 122888 | tf_op jit(solution)/shard_map/ppermute | solution.py:403
  45.7 5.0 %collective-permute-start.3 = (f32[5,8,2,128]{3,2,1,0:T(2,128)S(1)}, f32[5,8,2,128]{3,2,1,0:T(2,128)S(1)}, u32[]{:S(2)}, u32[]{:S(2)}) collective-permute-start(f32[5,8,2,128]{3,2,1,0:T(2,128)S(1)} %get-tuple-element.10), channel_id=1, source_target_pairs={{0,1},{2,3},{1,0},{3,2},{4,5},{6,7},{5,4},{7,6},{8,9},{10,11},{9,8... | collective-permute-start | bytes 122888 | tf_op jit(solution)/shard_map/ppermute | solution.py:404
